TPU v7x, 32 devices: a whole 2x2x4 slice. The times are simulated.
32 devices in a mesh: blk: 8 (over z, x), grp: 4 (over y, core).
Axes of the slice: x: 2, y: 2, z: 4, core: 2. Of those that a mesh axis runs over, the one named last changes fastest.
Arguments:
- image: bfloat16 [4, 8, 32768], P('grp', 'blk'), may hold values from -6 to 6
- context: bfloat16 [4, 1024, 128], P('grp'), may hold values from -6 to 6
- tissue: int32 [4, 8], P('grp'), may hold values from 0 to 15, as said below
- owner: int32 [4, 8], P('grp'), may hold values from 0 to 7, as said below
- neighbours: int32 [4, 8, 6], P('grp', 'blk'), may hold values from -1 to 7, as said below
- w_in: bfloat16 [7, 64, 1], replicated, may hold values from -2 to 2
- b_in: float32 [64], replicated, may hold values from -1.75 to 1.75
- w_down: bfloat16 [7, 128, 64], replicated, may hold values from -0.25 to 0.25
- b_down: float32 [128], replicated, may hold values from -1.75 to 1.75
- w_ctx: bfloat16 [7, 128, 128], replicated, may hold values from -0.1875 to 0.1875
- w_mid: bfloat16 [7, 128, 128], replicated, may hold values from -0.1875 to 0.1875
- b_mid: float32 [128], replicated, may hold values from -1.75 to 1.75
- w_skip: bfloat16 [128, 64], replicated, may hold values from -0.4375 to 0.4375
- w_lift: bfloat16 [128, 128], replicated, may hold values from -0.4375 to 0.4375
- b_up: float32 [128], replicated, may hold values from -1.75 to 1.75
- w_out: bfloat16 [3, 128], replicated, may hold values from -1 to 1
- b_out: float32 [3], replicated, may hold values from -3 to 3
Outputs:
- affinity: float32 [4, 8, 3, 32768], P('grp', 'blk')
Inputs may be any that keep to these rules, and one draw needn't show every extreme that they name: tissue[g] is the 8 consecutive positions of two adjacent x layers of section g. owner[g, j] = (j + r_g) mod 8 for a shift r_g of section g. neighbours[g, d, k] is the owner of the kept block next to device d's block in direction k within section g, -1 where that position is outside the section or not kept.
All inputs are finite; a program needn't handle non-finite values.
Results may differ from a plain program's by a relative error of at most 0.004.
Values may be sent and summed in bfloat16 or wider, within the bound.
No kernel may reach another device: no remote copies, remote signals or barrier semaphores. Data moves between devices by JAX's collectives and lax.ppermute only.
A program may use at most 64 MiB of HBM per device.

v0:
```python
import jax
import jax.numpy as jnp
from jax import lax
from jax.sharding import PartitionSpec as P

E = 32


def from_behind(shard, axis, by):
    devices = lax.axis_size(axis)
    return lax.ppermute(shard, axis, [(i, (i + by) % devices) for i in range(devices)])


def extended(shard, sides, width):
    for axis, dim in sides:
        devices, length = (lax.axis_size(axis), shard.shape[dim])
        up = [(i, (i + 1) % devices) for i in range(devices - 1)]
        down = [(j, i) for i, j in up]
        last = lax.slice_in_dim(shard, length - width, length, axis=dim)
        initial = lax.slice_in_dim(shard, 0, width, axis=dim)
        before = lax.ppermute(last, axis, up)
        after = lax.ppermute(initial, axis, down)
        shard = jnp.concatenate([before, shard, after], axis=dim)
    return shard


def faces_of(x):
    return jnp.stack([x[:, 0], x[:, -1], x[:, :, 0], x[:, :, -1], x[:, :, :, 0], x[:, :, :, -1]])


def conv_taps(x, halos, weight):
    chans = x.shape[0]
    views = [
        x,
        jnp.concatenate([halos[0][:, None], x[:, :-1]], 1),
        jnp.concatenate([x[:, 1:], halos[1][:, None]], 1),
        jnp.concatenate([halos[2][:, :, None], x[:, :, :-1]], 2),
        jnp.concatenate([x[:, :, 1:], halos[3][:, :, None]], 2),
        jnp.concatenate([halos[4][:, :, :, None], x[:, :, :, :-1]], 3),
        jnp.concatenate([x[:, :, :, 1:], halos[5][:, :, :, None]], 3),
    ]
    total = jnp.dot(weight[0], views[0].reshape(chans, -1), preferred_element_type=jnp.float32)
    for tap in range(1, 7):
        total = total + jnp.dot(
            weight[tap], views[tap].reshape(chans, -1), preferred_element_type=jnp.float32
        )
    return total


def upsample(v, factor):
    chans, side = (v.shape[0], v.shape[1])
    big = jnp.broadcast_to(
        v[:, :, None, :, None, :, None], (chans, side, factor, side, factor, side, factor)
    )
    return big.reshape(chans, side * factor, side * factor, side * factor)


def pooled(a0):
    half = a0.shape[1] // 2
    return a0.reshape(a0.shape[0], half, 2, half, 2, half, 2).max(axis=(2, 4, 6))


def neighbour_faces(x, nbr):
    flat = faces_of(x)
    count = lax.axis_size("blk")
    depth_blocks = count // 8
    offsets = [-(count // 2), count // 2, -depth_blocks, depth_blocks, -1, 1]
    pieces = []
    for direction in range(6):
        pieces.append(from_behind(flat[direction ^ 1], "blk", -offsets[direction]))
    mask = (nbr >= 0).astype(jnp.bfloat16)
    return jnp.stack(pieces) * mask[:, None, None, None]


def context_term(near, bx, by, bz, w_ctx, coarse, depth_blocks):
    side = 4 * coarse
    chans = near.shape[-1]
    regions = near.reshape(3, side, side, depth_blocks * coarse, chans)
    middle = jnp.pad(regions[1], ((coarse, coarse), (coarse, coarse), (0, 0), (0, 0)))
    zoff = bz * coarse
    xoff = bx * coarse
    yoff = by * coarse
    zero = jnp.zeros((), jnp.int32)
    size = (coarse, coarse, coarse, chans)
    shift = jnp.int32(coarse)
    taps = [
        lax.dynamic_slice(middle, (xoff + shift, yoff + shift, zoff, zero), size),
        lax.dynamic_slice(middle, (xoff, yoff + shift, zoff, zero), size),
        lax.dynamic_slice(middle, (xoff + 2 * shift, yoff + shift, zoff, zero), size),
        lax.dynamic_slice(middle, (xoff + shift, yoff, zoff, zero), size),
        lax.dynamic_slice(middle, (xoff + shift, yoff + 2 * shift, zoff, zero), size),
        lax.dynamic_slice(regions[0], (xoff, yoff, zoff, zero), size),
        lax.dynamic_slice(regions[2], (xoff, yoff, zoff, zero), size),
    ]
    total = jnp.dot(taps[0].reshape(-1, chans), w_ctx[0], preferred_element_type=jnp.float32)
    for tap in range(1, 7):
        total = total + jnp.dot(
            taps[tap].reshape(-1, chans), w_ctx[tap], preferred_element_type=jnp.float32
        )
    return total.T.reshape(-1, coarse, coarse, coarse)


def shards(
    image,
    context,
    tissue,
    owner,
    neighbours,
    w_in,
    b_in,
    w_down,
    b_down,
    w_ctx,
    w_mid,
    b_mid,
    w_skip,
    w_lift,
    b_up,
    w_out,
    b_out,
):
    half = E // 2
    coarse = E // 8
    depth_blocks = tissue.shape[1] // 8
    nbr = neighbours[0, 0]
    volume = image.reshape(1, E, E, E)
    pre = conv_taps(volume, neighbour_faces(volume, nbr), w_in) + b_in[:, None]
    a0 = jnp.maximum(pre, 0.0).astype(jnp.bfloat16).reshape(-1, E, E, E)
    p1 = pooled(a0)
    pre = conv_taps(p1, neighbour_faces(p1, nbr), w_down) + b_down[:, None]
    a1 = jnp.maximum(pre, 0.0).astype(jnp.bfloat16).reshape(-1, half, half, half)
    me = lax.axis_index("blk")
    pos = jnp.sum(jnp.where(owner[0] == me, tissue[0], 0))
    bx = pos // (4 * depth_blocks)
    by = pos // depth_blocks % 4
    bz = pos % depth_blocks
    near = extended(context, (("grp", 0),), 1)
    cterm = context_term(near, bx, by, bz, w_ctx, coarse, depth_blocks)
    pre = conv_taps(a1, neighbour_faces(a1, nbr), w_mid) + b_mid[:, None]
    pre = pre + upsample(cterm, 4).reshape(cterm.shape[0], -1)
    a2 = jnp.maximum(pre, 0.0).astype(jnp.bfloat16)
    lifted = jnp.dot(w_lift, a2, preferred_element_type=jnp.float32).reshape(-1, half, half, half)
    mixed = upsample(lifted, 2).reshape(lifted.shape[0], -1)
    mixed = (
        mixed
        + jnp.dot(w_skip, a0.reshape(a0.shape[0], -1), preferred_element_type=jnp.float32)
        + b_up[:, None]
    )
    hidden = jnp.maximum(mixed, 0.0).astype(jnp.bfloat16)
    logits = jnp.dot(w_out, hidden, preferred_element_type=jnp.float32) + b_out[:, None]
    return jax.nn.sigmoid(logits).reshape(1, 1, 3, E * E * E)


def solution(mesh):
    return jax.shard_map(
        shards,
        mesh=mesh,
        in_specs=(
            P("grp", "blk", None),
            P("grp", None, None),
            P("grp", None),
            P("grp", None),
            P("grp", "blk", None),
            P(),
            P(),
            P(),
            P(),
            P(),
            P(),
            P(),
            P(),
            P(),
            P(),
            P(),
            P(),
        ),
        out_specs=P("grp", "blk", None, None),
        check_vma=False,
    )
```

profile of v0, /device:TPU:0, one launch (start us, length us, event | category | flops | bytes accessed | tf_op | source)
XLA Modules:
  0.0 189.7 jit_solution(13854350175074094951)
XLA Ops:
  0.0 1.4 collective-permute-start.19
  1.4 3.7 %collective-permute-start.18 = (bf16[1,1024,128]{2,1,0:T(8,128)(2,1)}, bf16[1,1024,128]{2,1,0:T(8,128)(2,1)}, u32[]{:S(2)}, u32[]{:S(2)}) collective-permute-start(bf16[1,1024,128]{2,1,0:T(8,128)(2,1)} %param.18), channel_id=1, source_target_pairs={{0,1},{1,2},{2,3},{4,5},{5,6},{6,7},{8,9},{9,10},{10,11},{12,13},{... | collective-permute-start | bytes 786440 | tf_op jit(solution)/shard_map/ppermute | solution.py:21
  5.2 1.9 fusion.91
  7.2 4.1 %collective-permute-start.1 = (bf16[1,32,32]{2,1,0:T(8,128)(2,1)S(1)}, bf16[1,32,32]{2,1,0:T(8,128)(2,1)S(1)}, u32[]{:S(2)}, u32[]{:S(2)}) collective-permute-start(bf16[1,32,32]{2,1,0:T(8,128)(2,1)S(1)} %get-tuple-element.51), channel_id=1, source_target_pairs={{0,16},{4,20},{8,24},{12,28},{16,0},{20,4},{24,8},{28,12},{1,17},{... | collective-permute-start | bytes 6152 | tf_op jit(solution)/shard_map/ppermute | solution.py:11
  11.5 1.8 collective-permute-start.2
  13.3 1.4 fusion.73
  17.9 0.9 bitcast_convert_fusion.6
  20.6 0.9 convolution_add_fusion.17
  21.5 0.9 convolution_add_fusion.16
  25.4 3.1 %collective-permute-start.3 = (bf16[1,32,32]{2,1,0:T(8,128)(2,1)S(1)}, bf16[1,32,32]{2,1,0:T(8,128)(2,1)S(1)}, u32[]{:S(2)}, u32[]{:S(2)}) collective-permute-start(bf16[1,32,32]{2,1,0:T(8,128)(2,1)S(1)} %bitcast.402), channel_id=1, source_target_pairs={{0,28},{4,0},{8,4},{12,8},{16,12},{20,16},{24,20},{28,24},{1,29},{... | collective-permute-start | bytes 6152 | tf_op jit(solution)/shard_map/ppermute | solution.py:11
  28.5 4.7 %collective-permute-start.5 = (bf16[1,32,32]{2,1,0:T(8,128)(2,1)S(1)}, bf16[1,32,32]{2,1,0:T(8,128)(2,1)S(1)}, u32[]{:S(2)}, u32[]{:S(2)}) collective-permute-start(bf16[1,32,32]{2,1,0:T(8,128)(2,1)S(1)} %bitcast.400), channel_id=1, source_target_pairs={{0,28},{4,0},{8,4},{12,8},{16,12},{20,16},{24,20},{28,24},{1,29},{... | collective-permute-start | bytes 6152 | tf_op jit(solution)/shard_map/ppermute | solution.py:11
  33.2 1.6 collective-permute-done.4
  37.3 34.8 %fusion.11 = bf16[64,32768]{0,1:T(8,128)(2,1)} fusion(f32[64]{0:T(128)S(1)} %copy-done.14, f32[64]{0:T(128)S(1)} %get-tuple-element.71, f32[32768]{0:T(1024)S(1)} %reshape.336, f32[64]{0:T(128)S(1)} %get-tuple-element.72, f32[32768]{0:T(1024)S(1)} %reshape.334, f32[64]{0:T(128)S(1)} %get-tuple-element.67, f32[32768]{0:T(1024)S(1)} %reshape.332, ...), kind=kLoop, calls=%fused_computation.14 | loop fusion | flops 33554432 | bytes 5113856 | tf_op jit(solution)/shard_map/convert_element_type | solution.py:128
  72.2 13.6 %reduce_max.9 = bf16[64,16,16,16]{0,3,2,1:T(8,128)(2,1)S(1)} reduce(bf16[64,16,2,16,2,16,2]{0,6,5,4,3,2,1:T(2,128)(2,1)} %bitcast.368, bf16[]{:T(256)} %constant.63.clone.1), dimensions={2,4,6}, to_apply=%region_0.0 | reduce | flops 1835008 | bytes 4718594 | tf_op jit(solution)/shard_map/reduce_max | solution.py:60
  87.8 4.8 %collective-permute-start.9 = (bf16[64,16,16]{0,2,1:T(8,128)(2,1)S(1)}, bf16[64,16,16]{0,2,1:T(8,128)(2,1)S(1)}, u32[]{:S(2)}, u32[]{:S(2)}) collective-permute-start(bf16[64,16,16]{0,2,1:T(8,128)(2,1)S(1)} %get-tuple-element.25), channel_id=1, source_target_pairs={{0,28},{4,0},{8,4},{12,8},{16,12},{20,16},{24,20},{28,24},{1,29},{... | collective-permute-start | bytes 98312 | tf_op jit(solution)/shard_map/ppermute | solution.py:11
  92.6 2.1 %collective-permute-start.7 = (bf16[64,16,16]{0,2,1:T(8,128)(2,1)S(1)}, bf16[64,16,16]{0,2,1:T(8,128)(2,1)S(1)}, u32[]{:S(2)}, u32[]{:S(2)}) collective-permute-start(bf16[64,16,16]{0,2,1:T(8,128)(2,1)S(1)} %get-tuple-element.27), channel_id=1, source_target_pairs={{0,16},{4,20},{8,24},{12,28},{16,0},{20,4},{24,8},{28,12},{1,17},{... | collective-permute-start | bytes 98312 | tf_op jit(solution)/shard_map/ppermute | solution.py:11
  94.7 3.2 %collective-permute-done.7 = bf16[64,16,16]{0,2,1:T(8,128)(2,1)S(1)} collective-permute-done((bf16[64,16,16]{0,2,1:T(8,128)(2,1)S(1)}, bf16[64,16,16]{0,2,1:T(8,128)(2,1)S(1)}, u32[]{:S(2)}, u32[]{:S(2)}) %collective-permute-start.7) | collective-permute-done | bytes 32800 | tf_op jit(solution)/shard_map/ppermute | solution.py:11
  98.4 1.2 collective-permute-done.8
  99.6 3.7 %collective-permute-start.11 = (bf16[64,16,16]{0,2,1:T(8,128)(2,1)S(1)}, bf16[64,16,16]{0,2,1:T(8,128)(2,1)S(1)}, u32[]{:S(2)}, u32[]{:S(2)}) collective-permute-start(bf16[64,16,16]{0,2,1:T(8,128)(2,1)S(1)} %bitcast.388), channel_id=1, source_target_pairs={{0,28},{4,0},{8,4},{12,8},{16,12},{20,16},{24,20},{28,24},{1,29},{... | collective-permute-start | bytes 98312 | tf_op jit(solution)/shard_map/ppermute | solution.py:11
  103.3 1.9 %collective-permute-done.10 = bf16[64,16,16]{0,2,1:T(8,128)(2,1)S(1)} collective-permute-done((bf16[64,16,16]{0,2,1:T(8,128)(2,1)S(1)}, bf16[64,16,16]{0,2,1:T(8,128)(2,1)S(1)}, u32[]{:S(2)}, u32[]{:S(2)}) %collective-permute-start.10) | collective-permute-done | bytes 32800 | tf_op jit(solution)/shard_map/ppermute | solution.py:11
  112.7 2.4 %collective-permute-start.13 = (bf16[128,16,16]{0,2,1:T(8,128)(2,1)S(1)}, bf16[128,16,16]{0,2,1:T(8,128)(2,1)S(1)}, u32[]{:S(2)}, u32[]{:S(2)}) collective-permute-start(bf16[128,16,16]{0,2,1:T(8,128)(2,1)S(1)} %get-tuple-element.15), channel_id=1, source_target_pairs={{0,16},{4,20},{8,24},{12,28},{16,0},{20,4},{24,8},{28,12},{1,17},{... | collective-permute-start | bytes 196616 | tf_op jit(solution)/shard_map/ppermute | solution.py:11
  115.1 4.9 %collective-permute-start.15 = (bf16[128,16,16]{0,2,1:T(8,128)(2,1)S(1)}, bf16[128,16,16]{0,2,1:T(8,128)(2,1)S(1)}, u32[]{:S(2)}, u32[]{:S(2)}) collective-permute-start(bf16[128,16,16]{0,2,1:T(8,128)(2,1)S(1)} %get-tuple-element.13), channel_id=1, source_target_pairs={{0,28},{4,0},{8,4},{12,8},{16,12},{20,16},{24,20},{28,24},{1,29},{... | collective-permute-start | bytes 196616 | tf_op jit(solution)/shard_map/ppermute | solution.py:11
  120.3 6.8 %collective-permute-done.14 = bf16[128,16,16]{0,2,1:T(8,128)(2,1)S(1)} collective-permute-done((bf16[128,16,16]{0,2,1:T(8,128)(2,1)S(1)}, bf16[128,16,16]{0,2,1:T(8,128)(2,1)S(1)}, u32[]{:S(2)}, u32[]{:S(2)}) %collective-permute-start.14) | collective-permute-done | bytes 65568 | tf_op jit(solution)/shard_map/ppermute | solution.py:11
  127.1 0.9 collective-permute-start.17
  128.1 3.3 %collective-permute-done.17 = bf16[128,16,16]{0,2,1:T(8,128)(2,1)S(1)} collective-permute-done((bf16[128,16,16]{0,2,1:T(8,128)(2,1)S(1)}, bf16[128,16,16]{0,2,1:T(8,128)(2,1)S(1)}, u32[]{:S(2)}, u32[]{:S(2)}) %collective-permute-start.17) | collective-permute-done | bytes 65568 | tf_op jit(solution)/shard_map/ppermute | solution.py:11
  134.9 1.8 convolution_add_fusion.2
  138.3 0.9 fusion.21
  139.2 1.7 broadcast_in_dim.14
  140.9 3.1 %fusion.20 = f32[4096,128]{1,0:T(8,128)S(1)} fusion(bf16[128,128]{1,0:T(8,128)(2,1)S(1)} %copy-done, f32[128,4096]{0,1:T(8,128)} %bitcast.371, f32[4096,128]{1,0:T(8,128)} %convolution_add_fusion.2, bf16[128,4096]{0,1:T(8,128)(2,1)S(1)} %bitcast.383, f32[128]{0:T(128)S(1)} %copy-done.15, bf16[7,128,128]{2,1,0:T(8,128)(2,1)} %param.27), kind=kOutput, calls=%fused_computation.40 | convolution fusion | flops 271056896 | bytes 7406080 | tf_op jit(solution)/shard_map/dot_general | solution.py:142
  144.1 9.5 %broadcast_in_dim.30 = f32[128,16,2,16,2,16,2]{0,6,5,4,3,2,1:T(2,128)} broadcast(f32[128,16,16,16]{0,3,2,1:T(8,128)S(1)} %bitcast.370), dimensions={0,1,3,5} | broadcast | bytes 18874368 | tf_op jit(solution)/shard_map/broadcast_in_dim | solution.py:52
  153.7 34.8 %fusion.8 = f32[1,1,3,32768]{3,2,1,0:T(4,128)S(1)} fusion(bf16[3,128]{1,0:T(4,128)(2,1)S(1)} %copy-done.17, f32[128,32768]{0,1:T(8,128)} %bitcast.369, bf16[128,64]{0,1:T(8,128)(2,1)S(1)} %copy-done.16, f32[128]{0:T(128)S(1)} %copy-done.18, f32[3]{0:T(128)S(1)} %copy-done.19, f32[64]{0:T(128)S(1)} %copy-done.14, f32[64]{0:T(128)S(1)} %get-tuple-element.71, ...), kind=kOutput, calls=%fused_computation.10 | convolution fusion | flops 612761600 | bytes 18107660 | tf_op jit(solution)/shard_map/dot_general | solution.py:150
  188.5 1.2 copy.238
  (161 shorter events, 23.0 us)
Async XLA Ops:
  0.0 140.9 %copy-start = (bf16[128,128]{1,0:T(8,128)(2,1)S(1)}, bf16[128,128]{1,0:T(8,128)(2,1)}, u32[]{:S(2)}) copy-start(bf16[128,128]{1,0:T(8,128)(2,1)} %param.30) | copy-start | bytes 98308
  0.0 37.3 %copy-start.14 = (f32[64]{0:T(128)S(1)}, f32[64]{0:T(128)}, u32[]{:S(2)}) copy-start(f32[64]{0:T(128)} %param.23) | copy-start | bytes 772
  0.0 136.7 %collective-permute-start.19 = (bf16[1,1024,128]{2,1,0:T(8,128)(2,1)}, bf16[1,1024,128]{2,1,0:T(8,128)(2,1)}, u32[]{:S(2)}, u32[]{:S(2)}) collective-permute-start(bf16[1,1024,128]{2,1,0:T(8,128)(2,1)} %param.18), channel_id=1, source_target_pairs={{1,0},{2,1},{3,2},{5,4},{6,5},{7,6},{9,8},{10,9},{11,10},{13,12},{... | collective-permute-start | bytes 786440 | tf_op jit(solution)/shard_map/ppermute | solution.py:22
  1.4 135.3 %collective-permute-start.18 = (bf16[1,1024,128]{2,1,0:T(8,128)(2,1)}, bf16[1,1024,128]{2,1,0:T(8,128)(2,1)}, u32[]{:S(2)}, u32[]{:S(2)}) collective-permute-start(bf16[1,1024,128]{2,1,0:T(8,128)(2,1)} %param.18), channel_id=1, source_target_pairs={{0,1},{1,2},{2,3},{4,5},{5,6},{6,7},{8,9},{9,10},{10,11},{12,13},{... | collective-permute-start | bytes 786440 | tf_op jit(solution)/shard_map/ppermute | solution.py:21
  7.2 21.2 %collective-permute-start.1 = (bf16[1,32,32]{2,1,0:T(8,128)(2,1)S(1)}, bf16[1,32,32]{2,1,0:T(8,128)(2,1)S(1)}, u32[]{:S(2)}, u32[]{:S(2)}) collective-permute-start(bf16[1,32,32]{2,1,0:T(8,128)(2,1)S(1)} %get-tuple-element.51), channel_id=1, source_target_pairs={{0,16},{4,20},{8,24},{12,28},{16,0},{20,4},{24,8},{28,12},{1,17},{... | collective-permute-start | bytes 6152 | tf_op jit(solution)/shard_map/ppermute | solution.py:11
  11.4 14.0 %collective-permute-start = (bf16[1,32,32]{2,1,0:T(8,128)(2,1)S(1)}, bf16[1,32,32]{2,1,0:T(8,128)(2,1)S(1)}, u32[]{:S(2)}, u32[]{:S(2)}) collective-permute-start(bf16[1,32,32]{2,1,0:T(8,128)(2,1)S(1)} %get-tuple-element.52), channel_id=1, source_target_pairs={{0,16},{4,20},{8,24},{12,28},{16,0},{20,4},{24,8},{28,12},{1,17},{... | collective-permute-start | bytes 6152 | tf_op jit(solution)/shard_map/ppermute | solution.py:11
  11.5 17.0 %collective-permute-start.2 = (bf16[1,32,32]{2,1,0:T(8,128)(2,1)S(1)}, bf16[1,32,32]{2,1,0:T(8,128)(2,1)S(1)}, u32[]{:S(2)}, u32[]{:S(2)}) collective-permute-start(bf16[1,32,32]{2,1,0:T(8,128)(2,1)S(1)} %bitcast.399), channel_id=1, source_target_pairs={{0,4},{4,8},{8,12},{12,16},{16,20},{20,24},{24,28},{28,0},{1,5},{5... | collective-permute-start | bytes 6152 | tf_op jit(solution)/shard_map/ppermute | solution.py:11
  25.4 7.8 %collective-permute-start.3 = (bf16[1,32,32]{2,1,0:T(8,128)(2,1)S(1)}, bf16[1,32,32]{2,1,0:T(8,128)(2,1)S(1)}, u32[]{:S(2)}, u32[]{:S(2)}) collective-permute-start(bf16[1,32,32]{2,1,0:T(8,128)(2,1)S(1)} %bitcast.402), channel_id=1, source_target_pairs={{0,28},{4,0},{8,4},{12,8},{16,12},{20,16},{24,20},{28,24},{1,29},{... | collective-permute-start | bytes 6152 | tf_op jit(solution)/shard_map/ppermute | solution.py:11
  28.5 6.3 %collective-permute-start.4 = (bf16[1,32,32]{2,1,0:T(8,128)(2,1)S(1)}, bf16[1,32,32]{2,1,0:T(8,128)(2,1)S(1)}, u32[]{:S(2)}, u32[]{:S(2)}) collective-permute-start(bf16[1,32,32]{2,1,0:T(8,128)(2,1)S(1)} %bitcast.401), channel_id=1, source_target_pairs={{0,4},{4,8},{8,12},{12,16},{16,20},{20,24},{24,28},{28,0},{1,5},{5... | collective-permute-start | bytes 6152 | tf_op jit(solution)/shard_map/ppermute | solution.py:11
  28.5 6.3 %collective-permute-start.5 = (bf16[1,32,32]{2,1,0:T(8,128)(2,1)S(1)}, bf16[1,32,32]{2,1,0:T(8,128)(2,1)S(1)}, u32[]{:S(2)}, u32[]{:S(2)}) collective-permute-start(bf16[1,32,32]{2,1,0:T(8,128)(2,1)S(1)} %bitcast.400), channel_id=1, source_target_pairs={{0,28},{4,0},{8,4},{12,8},{16,12},{20,16},{24,20},{28,24},{1,29},{... | collective-permute-start | bytes 6152 | tf_op jit(solution)/shard_map/ppermute | solution.py:11
  36.6 49.2 %copy-start.2 = (f32[32768]{0:T(1024)}, f32[32768]{0:T(1024)S(1)}, u32[]{:S(2)}) copy-start(f32[32768]{0:T(1024)S(1)} %reshape.330) | copy-start | bytes 393220
  36.8 49.0 %copy-start.4 = (f32[32768]{0:T(1024)}, f32[32768]{0:T(1024)S(1)}, u32[]{:S(2)}) copy-start(f32[32768]{0:T(1024)S(1)} %reshape.332) | copy-start | bytes 393220
  37.1 48.6 %copy-start.6 = (f32[32768]{0:T(1024)}, f32[32768]{0:T(1024)S(1)}, u32[]{:S(2)}) copy-start(f32[32768]{0:T(1024)S(1)} %reshape.326) | copy-start | bytes 393220
  37.3 34.9 %copy-start.8 = (f32[32768]{0:T(1024)}, f32[32768]{0:T(1024)S(1)}, u32[]{:S(2)}) copy-start(f32[32768]{0:T(1024)S(1)} %reshape.328) | copy-start | bytes 393220
  87.2 5.3 %collective-permute-start.6 = (bf16[64,16,16]{0,2,1:T(8,128)(2,1)S(1)}, bf16[64,16,16]{0,2,1:T(8,128)(2,1)S(1)}, u32[]{:S(2)}, u32[]{:S(2)}) collective-permute-start(bf16[64,16,16]{0,2,1:T(8,128)(2,1)S(1)} %get-tuple-element.28), channel_id=1, source_target_pairs={{0,16},{4,20},{8,24},{12,28},{16,0},{20,4},{24,8},{28,12},{1,17},{... | collective-permute-start | bytes 98312 | tf_op jit(solution)/shard_map/ppermute | solution.py:11
  87.8 15.5 %collective-permute-start.9 = (bf16[64,16,16]{0,2,1:T(8,128)(2,1)S(1)}, bf16[64,16,16]{0,2,1:T(8,128)(2,1)S(1)}, u32[]{:S(2)}, u32[]{:S(2)}) collective-permute-start(bf16[64,16,16]{0,2,1:T(8,128)(2,1)S(1)} %get-tuple-element.25), channel_id=1, source_target_pairs={{0,28},{4,0},{8,4},{12,8},{16,12},{20,16},{24,20},{28,24},{1,29},{... | collective-permute-start | bytes 98312 | tf_op jit(solution)/shard_map/ppermute | solution.py:11
  92.5 7.0 %collective-permute-start.8 = (bf16[64,16,16]{0,2,1:T(8,128)(2,1)S(1)}, bf16[64,16,16]{0,2,1:T(8,128)(2,1)S(1)}, u32[]{:S(2)}, u32[]{:S(2)}) collective-permute-start(bf16[64,16,16]{0,2,1:T(8,128)(2,1)S(1)} %get-tuple-element.26), channel_id=1, source_target_pairs={{0,4},{4,8},{8,12},{12,16},{16,20},{20,24},{24,28},{28,0},{1,5},{5... | collective-permute-start | bytes 98312 | tf_op jit(solution)/shard_map/ppermute | solution.py:11
  92.6 5.2 %collective-permute-start.7 = (bf16[64,16,16]{0,2,1:T(8,128)(2,1)S(1)}, bf16[64,16,16]{0,2,1:T(8,128)(2,1)S(1)}, u32[]{:S(2)}, u32[]{:S(2)}) collective-permute-start(bf16[64,16,16]{0,2,1:T(8,128)(2,1)S(1)} %get-tuple-element.27), channel_id=1, source_target_pairs={{0,16},{4,20},{8,24},{12,28},{16,0},{20,4},{24,8},{28,12},{1,17},{... | collective-permute-start | bytes 98312 | tf_op jit(solution)/shard_map/ppermute | solution.py:11
  97.8 7.4 %collective-permute-start.10 = (bf16[64,16,16]{0,2,1:T(8,128)(2,1)S(1)}, bf16[64,16,16]{0,2,1:T(8,128)(2,1)S(1)}, u32[]{:S(2)}, u32[]{:S(2)}) collective-permute-start(bf16[64,16,16]{0,2,1:T(8,128)(2,1)S(1)} %bitcast.390), channel_id=1, source_target_pairs={{0,4},{4,8},{8,12},{12,16},{16,20},{20,24},{24,28},{28,0},{1,5},{5... | collective-permute-start | bytes 98312 | tf_op jit(solution)/shard_map/ppermute | solution.py:11
  99.6 5.7 %collective-permute-start.11 = (bf16[64,16,16]{0,2,1:T(8,128)(2,1)S(1)}, bf16[64,16,16]{0,2,1:T(8,128)(2,1)S(1)}, u32[]{:S(2)}, u32[]{:S(2)}) collective-permute-start(bf16[64,16,16]{0,2,1:T(8,128)(2,1)S(1)} %bitcast.388), channel_id=1, source_target_pairs={{0,28},{4,0},{8,4},{12,8},{16,12},{20,16},{24,20},{28,24},{1,29},{... | collective-permute-start | bytes 98312 | tf_op jit(solution)/shard_map/ppermute | solution.py:11
  111.6 8.5 %collective-permute-start.12 = (bf16[128,16,16]{0,2,1:T(8,128)(2,1)S(1)}, bf16[128,16,16]{0,2,1:T(8,128)(2,1)S(1)}, u32[]{:S(2)}, u32[]{:S(2)}) collective-permute-start(bf16[128,16,16]{0,2,1:T(8,128)(2,1)S(1)} %get-tuple-element.16), channel_id=1, source_target_pairs={{0,16},{4,20},{8,24},{12,28},{16,0},{20,4},{24,8},{28,12},{1,17},{... | collective-permute-start | bytes 196616 | tf_op jit(solution)/shard_map/ppermute | solution.py:11
  112.7 7.5 %collective-permute-start.13 = (bf16[128,16,16]{0,2,1:T(8,128)(2,1)S(1)}, bf16[128,16,16]{0,2,1:T(8,128)(2,1)S(1)}, u32[]{:S(2)}, u32[]{:S(2)}) collective-permute-start(bf16[128,16,16]{0,2,1:T(8,128)(2,1)S(1)} %get-tuple-element.15), channel_id=1, source_target_pairs={{0,16},{4,20},{8,24},{12,28},{16,0},{20,4},{24,8},{28,12},{1,17},{... | collective-permute-start | bytes 196616 | tf_op jit(solution)/shard_map/ppermute | solution.py:11
  115.1 12.9 %collective-permute-start.15 = (bf16[128,16,16]{0,2,1:T(8,128)(2,1)S(1)}, bf16[128,16,16]{0,2,1:T(8,128)(2,1)S(1)}, u32[]{:S(2)}, u32[]{:S(2)}) collective-permute-start(bf16[128,16,16]{0,2,1:T(8,128)(2,1)S(1)} %get-tuple-element.13), channel_id=1, source_target_pairs={{0,28},{4,0},{8,4},{12,8},{16,12},{20,16},{24,20},{28,24},{1,29},{... | collective-permute-start | bytes 196616 | tf_op jit(solution)/shard_map/ppermute | solution.py:11
  120.1 7.0 %collective-permute-start.14 = (bf16[128,16,16]{0,2,1:T(8,128)(2,1)S(1)}, bf16[128,16,16]{0,2,1:T(8,128)(2,1)S(1)}, u32[]{:S(2)}, u32[]{:S(2)}) collective-permute-start(bf16[128,16,16]{0,2,1:T(8,128)(2,1)S(1)} %get-tuple-element.14), channel_id=1, source_target_pairs={{0,4},{4,8},{8,12},{12,16},{16,20},{20,24},{24,28},{28,0},{1,5},{5... | collective-permute-start | bytes 196616 | tf_op jit(solution)/shard_map/ppermute | solution.py:11
  120.2 7.9 %collective-permute-start.16 = (bf16[128,16,16]{0,2,1:T(8,128)(2,1)S(1)}, bf16[128,16,16]{0,2,1:T(8,128)(2,1)S(1)}, u32[]{:S(2)}, u32[]{:S(2)}) collective-permute-start(bf16[128,16,16]{0,2,1:T(8,128)(2,1)S(1)} %bitcast.391), channel_id=1, source_target_pairs={{0,4},{4,8},{8,12},{12,16},{16,20},{20,24},{24,28},{28,0},{1,5},{5... | collective-permute-start | bytes 196616 | tf_op jit(solution)/shard_map/ppermute | solution.py:11
  127.1 4.3 %collective-permute-start.17 = (bf16[128,16,16]{0,2,1:T(8,128)(2,1)S(1)}, bf16[128,16,16]{0,2,1:T(8,128)(2,1)S(1)}, u32[]{:S(2)}, u32[]{:S(2)}) collective-permute-start(bf16[128,16,16]{0,2,1:T(8,128)(2,1)S(1)} %bitcast.389), channel_id=1, source_target_pairs={{0,28},{4,0},{8,4},{12,8},{16,12},{20,16},{24,20},{28,24},{1,29},{... | collective-permute-start | bytes 196616 | tf_op jit(solution)/shard_map/ppermute | solution.py:11
  144.0 9.6 %copy-start.3 = (f32[32768]{0:T(1024)S(1)}, f32[32768]{0:T(1024)}, u32[]{:S(2)}) copy-start(f32[32768]{0:T(1024)} %copy-done.2) | copy-start | bytes 393220
  144.0 9.6 %copy-start.5 = (f32[32768]{0:T(1024)S(1)}, f32[32768]{0:T(1024)}, u32[]{:S(2)}) copy-start(f32[32768]{0:T(1024)} %copy-done.4) | copy-start | bytes 393220
  144.0 9.6 %copy-start.7 = (f32[32768]{0:T(1024)S(1)}, f32[32768]{0:T(1024)}, u32[]{:S(2)}) copy-start(f32[32768]{0:T(1024)} %copy-done.6) | copy-start | bytes 393220
  144.0 9.6 %copy-start.9 = (f32[32768]{0:T(1024)S(1)}, f32[32768]{0:T(1024)}, u32[]{:S(2)}) copy-start(f32[32768]{0:T(1024)} %copy-done.8) | copy-start | bytes 393220
  144.0 9.6 %copy-start.10 = (f32[1,1,32768]{2,1,0:T(1,128)S(1)}, f32[1,1,32768]{2,1,0:T(1,128)}, u32[]{:S(2)}) copy-start(f32[1,1,32768]{2,1,0:T(1,128)} %get-tuple-element.58) | copy-start | bytes 393220
  153.7 36.0 %copy-start.1 = (bf16[128,128]{1,0:T(8,128)(2,1)S(1)}, bf16[128,128]{1,0:T(8,128)(2,1)}, u32[]{:S(2)}) copy-start(bf16[128,128]{1,0:T(8,128)(2,1)} %param.30) | copy-start | bytes 98308
  (8 other events, 51.8 us)
where the time goes:
time: 191 us; the launch traced here: 190 us
  other arithmetic  57.4 us (30%)
  matrix products  50.9 us (27%)
  starting transfers between devices  39.2 us (21%)
  local copies, waits for them, and re-layouts  20.5 us (11%)
  waiting for transfers between devices  18 us (9%)
  between operations  3.64 us (2%)
    convert_element_type x1, other arithmetic, shards(): a0 = jnp.maximum(pre, 0.0).astype(jnp.bfloat16).reshape(-1, E, E, E)  34.8 us
    dot_general x1, matrix products, shards(): jnp.dot(w_out, hidden, preferred_element_type=jnp.float32) + b_out[:, None]  34.8 us
    ppermute x18, starting transfers between devices, from_behind(): lax.ppermute(shard, axis, [(i, (i + by) % devices) for i in range(devices)])  34 us
    ppermute x18, waiting for transfers between devices, from_behind(): lax.ppermute(shard, axis, [(i, (i + by) % devices) for i in range(devices)])  18 us
    reduce_max x1, other arithmetic, pooled(): a0.reshape(a0.shape[0], half, 2, half, 2, half, 2).max(axis=(2, 4, 6))  13.6 us
    broadcast_in_dim x2, local copies, waits for them, and re-layouts, upsample(): jnp.broadcast_to(v[:, :, None, :, None, :, None], (chans, side, factor, s...  11.2 us
    dot_general x11, matrix products, conv_taps(): jnp.dot(weight[tap], views[tap].reshape(chans, -1), preferred_element_typ...  6.01 us
    dot_general x6, matrix products, context_term(): jnp.dot(taps[tap].reshape(-1, chans), w_ctx[tap], preferred_element_type=...  5.35 us
  transfers between devices with their start and end apart: 20, of which 6 were waited for; matrix products, arithmetic and copies ran while one was open for 40% of the time, Pallas kernels for 0%

commit v1 on v0

--- a/solution.py
+++ b/solution.py
@@ -1,6 +1,8 @@
 import jax
 import jax.numpy as jnp
 from jax import lax
+from jax.experimental import pallas as pl
+from jax.experimental.pallas import tpu as pltpu
 from jax.sharding import PartitionSpec as P
 
 E = 32
@@ -100,7 +102,7 @@
     return total.T.reshape(-1, coarse, coarse, coarse)
 
 
-def shards(
+def layered_shards(
     image,
     context,
     tissue,
@@ -151,9 +153,339 @@
     return jax.nn.sigmoid(logits).reshape(1, 1, 3, E * E * E)
 
 
+H = E // 2
+REACH = 8
+SLABS = H + 4
+WIDE = E + 2 * REACH
+
+
+def selections():
+    row = jnp.arange(8 * SLABS)
+    slab, kk = row // 8, row % 8
+    offset = jnp.where(kk < 4, kk - 1, kk % 2)
+    pick = 2 * (slab - 2) + offset + REACH
+    rows = (pick[:, None] == jnp.arange(WIDE)[None, :]).astype(jnp.bfloat16)
+    cell = jnp.arange(512)
+    y, z = cell // E, cell % E
+    to = ((y % 2) * 2 + z % 2) * 128 + (y // 2) * H + z // 2
+    split = (to[:, None] == cell[None, :]).astype(jnp.bfloat16)
+    return rows, split, split.T
+
+
+def input_taps(w_in):
+    table = [[-1] * 8 for _ in range(32)]
+    for p in range(8):
+        px, py, pz = p // 4, p // 2 % 2, p % 2
+        same = py * 2 + pz
+        other_y, other_z = (1 - py) * 2 + pz, py * 2 + 1 - pz
+        table[same * 8 + px + 1][p] = 0
+        table[same * 8 + px][p] = 1
+        table[same * 8 + px + 2][p] = 2
+        near_y, near_z = px + 1, px + 1
+        far_y, far_z = 4 + px, 6 + px
+        table[other_y * 8 + (far_y if py == 0 else near_y)][p] = 3
+        table[other_y * 8 + (near_y if py == 0 else far_y)][p] = 4
+        table[other_z * 8 + (far_z if pz == 0 else near_z)][p] = 5
+        table[other_z * 8 + (near_z if pz == 0 else far_z)][p] = 6
+    chans = w_in.shape[1]
+    tap = jnp.repeat(jnp.array(table, jnp.int32), chans, axis=1)
+    wide = jnp.tile(w_in[:, :, 0], (1, 8))
+    total = jnp.zeros((32, 8 * chans), jnp.bfloat16)
+    for t in range(7):
+        total = jnp.where(tap == t, wide[t][None, :], total)
+    return total
+
+
+def three_terms(v):
+    high = v.astype(jnp.bfloat16)
+    rest = v - high.astype(jnp.float32)
+    mid = rest.astype(jnp.bfloat16)
+    low = (rest - mid.astype(jnp.float32)).astype(jnp.bfloat16)
+    return high, mid, low
+
+
+def block_kernel(
+    s_ref, ex_ref, lo_ref, hi_ref, rows_ref, split_ref, join_ref, ctx_ref, below_ref, above_ref,
+    w1_ref, b1_ref, wd_ref, bd_ref, wc_ref, wm_ref, bm_ref, wp_ref, bp_ref, wo_ref, bo_ref,
+    out_ref,
+    g_ref, p_ref, a0_ref, p1_ref, a1_ref, k1_ref, kd_ref, ku_ref, l_ref,
+):
+    bf, f32 = jnp.bfloat16, jnp.float32
+    bx, by = s_ref[0], s_ref[1]
+    first, last = s_ref[2] > 0, s_ref[3] > 0
+    left, right = s_ref[4] > 0, s_ref[5] > 0
+
+    def iota(shape, dim):
+        return lax.broadcasted_iota(jnp.int32, shape, dim)
+
+    def dot(a, b):
+        return jnp.dot(a, b, preferred_element_type=f32)
+
+    k1_ref[0:32, :] = w1_ref[...]
+    k1_ref[32:48, :] = jnp.concatenate(
+        [t.astype(f32) for t in three_terms(b1_ref[...])] + [jnp.zeros((13, 512), f32)], axis=0
+    ).astype(bf)
+    kd_ref[0:448, :] = wd_ref[...]
+    kd_ref[448:512, :] = jnp.concatenate(
+        [t.astype(f32) for t in three_terms(bd_ref[...])] + [jnp.zeros((61, 128), f32)], axis=0
+    ).astype(bf)
+
+    def near(dx, dy):
+        x, y = bx + dx, by + dy
+        ok = (x >= 0) & (x < 4) & (y >= 0) & (y < 4)
+        x, y = jnp.clip(x, 0, 3), jnp.clip(y, 0, 3)
+        v = ctx_ref[pl.ds(4 * x, 4), pl.ds(y, 1), :, :].reshape(64, 128)
+        return jnp.where(ok, v, jnp.zeros_like(v))
+
+    views = [near(0, 0), near(-1, 0), near(1, 0), near(0, -1), near(0, 1)]
+    for other in (below_ref, above_ref):
+        views.append(other[pl.ds(4 * bx, 4), pl.ds(by, 1), :, :].reshape(64, 128))
+    total = dot(views[0], wc_ref[0])
+    for t in range(1, 7):
+        total = total + dot(views[t], wc_ref[t])
+    terms = three_terms(total)
+    bias = [t.astype(f32) for t in three_terms(bm_ref[...])]
+    for q in range(4):
+        ku_ref[q] = jnp.concatenate(
+            [t[16 * q : 16 * q + 16].astype(f32) for t in terms] + bias + [jnp.zeros((77, 128), f32)],
+            axis=0,
+        ).astype(bf)
+
+    field = jnp.concatenate([lo_ref[...], ex_ref[...], hi_ref[...]], axis=1)
+    field = dot(rows_ref[...], field).astype(bf)
+    for j in range(3):
+        part = dot(field[:, 512 * j : 512 * j + 512], split_ref[...])
+        for q in range(4):
+            g_ref[q, :, 128 * j : 128 * j + 128] = part[:, 128 * q : 128 * q + 128]
+    shape = (8 * SLABS, 384)
+    kk = iota(shape, 0) % 8
+    hz = iota(shape, 1) % H
+    for q in range(4):
+        py, pz = q // 2, q % 2
+        v = g_ref[q]
+        ys = pltpu.roll(v, H if py == 1 else 384 - H, axis=1)
+        zs = pltpu.roll(v, 1 if pz == 1 else 383, axis=1)
+        zs = jnp.where(hz == (0 if pz == 1 else H - 1), 0.0, zs)
+        v = jnp.where(kk < 4, v, jnp.where(kk < 6, ys, zs))
+        p_ref[:, 8 * q : 8 * q + 8, :] = v.reshape(SLABS, 8, 384)
+
+    ones = jnp.where(iota((16, 384), 0) < 3, 1.0, 0.0)
+    start = jnp.where(first, 0, 2)
+    p1_ref[0:2] = jnp.zeros((2, 320, 128), bf)
+    p1_ref[SLABS - 2 : SLABS] = jnp.zeros((2, 320, 128), bf)
+    a1_ref[0] = jnp.zeros((288, 128), bf)
+    a1_ref[H + 1] = jnp.zeros((288, 128), bf)
+
+    def full_res(i, carry):
+        s = start + i
+        taps = jnp.concatenate([p_ref[s], ones], axis=0)
+        taps = taps.T[32:352].astype(bf)
+        pre = dot(taps, k1_ref[...])
+        pool = jnp.maximum(
+            jnp.maximum(pre[:, 0:128], pre[:, 128:256]), jnp.maximum(pre[:, 256:384], pre[:, 384:512])
+        )
+        pool = jnp.maximum(pool, pltpu.roll(pool, 64, axis=1))
+        p1_ref[s] = jnp.maximum(pool, 0.0).astype(bf)
+
+        @pl.when(jnp.logical_not(left))
+        def _():
+            p1_ref[s, 0:32] = jnp.zeros((32, 128), bf)
+
+        @pl.when(jnp.logical_not(right))
+        def _():
+            p1_ref[s, 288:320] = jnp.zeros((32, 128), bf)
+
+        @pl.when((s >= 2) & (s < H + 2))
+        def _():
+            a0_ref[s - 2] = jnp.maximum(pre[32:288], 0.0).astype(bf)
+
+        return carry
+
+    lax.fori_loop(0, H + 2, full_res, 0)
+
+    lane = iota((288, 128), 1)
+    zrow = iota((288, 128), 0) % H
+    low = lane < 64
+    cut = zrow == jnp.where(low, 0, H - 1)
+    extra = jnp.where(lane < 67, 1.0, 0.0).astype(bf)
+    begin = jnp.where(first, 0, 1)
+
+    def half_res(i, carry):
+        u = begin + i
+        s = u + 1
+        mid = p1_ref[s, 16:304]
+        t1 = jnp.where(low, p1_ref[s - 1, 16:304], p1_ref[s + 1, 16:304])
+        t2 = jnp.where(low, p1_ref[s, 0:288], p1_ref[s, 32:320])
+        wide = mid.astype(f32)
+        t3 = jnp.where(low, pltpu.roll(wide, 1, axis=0), pltpu.roll(wide, 287, axis=0))
+        t3 = jnp.where(cut, 0.0, t3).astype(bf)
+        t4 = jnp.where(low, mid, extra)
+        pre = dot(jnp.concatenate([t1, t2], axis=1), kd_ref[0:256]) + dot(
+            jnp.concatenate([t3, t4], axis=1), kd_ref[256:512]
+        )
+        a1_ref[u] = jnp.maximum(pre, 0.0).astype(bf)
+
+        @pl.when(jnp.logical_not(left))
+        def _():
+            a1_ref[u, 0:16] = jnp.zeros((16, 128), bf)
+
+        @pl.when(jnp.logical_not(right))
+        def _():
+            a1_ref[u, 272:288] = jnp.zeros((16, 128), bf)
+
+        return carry
+
+    lax.fori_loop(0, H + 1, half_res, 0)
+
+    rows = iota((256, 128), 0)
+    cols = iota((256, 128), 1)
+    coarse = (rows // H) // 4 * 4 + rows % H // 4
+    spread = jnp.where(cols < 48, jnp.where(cols % H == coarse, 1.0, 0.0), jnp.where(cols < 51, 1.0, 0.0))
+    spread = spread.astype(bf)
+    zfirst, zlast = rows % H == 0, rows % H == H - 1
+
+    def decode(h, carry):
+        u = h + 1
+        mid = a1_ref[u, 16:272]
+        wide = mid.astype(f32)
+        zm = jnp.where(zfirst, 0.0, pltpu.roll(wide, 1, axis=0)).astype(bf)
+        zp = jnp.where(zlast, 0.0, pltpu.roll(wide, 255, axis=0)).astype(bf)
+        pre = dot(jnp.concatenate([a1_ref[u - 1, 16:272], a1_ref[u + 1, 16:272]], axis=1), wm_ref[0:256])
+        pre = pre + dot(jnp.concatenate([a1_ref[u, 0:256], a1_ref[u, 32:288]], axis=1), wm_ref[256:512])
+        pre = pre + dot(jnp.concatenate([zm, zp], axis=1), wm_ref[512:768])
+        kc = jnp.concatenate([wm_ref[768:896], ku_ref[h // 4]], axis=0)
+        pre = pre + dot(jnp.concatenate([mid, spread], axis=1), kc)
+        a2 = jnp.maximum(pre, 0.0).astype(bf)
+        logits = None
+        for m in range(4):
+            both = jnp.concatenate([a0_ref[h, :, 128 * m : 128 * m + 128], a2], axis=1)
+            mixed = dot(both, wp_ref[...]) + bp_ref[...]
+            hidden = jnp.maximum(mixed, 0.0).astype(bf)
+            part = lax.dot_general(
+                wo_ref[m], hidden, (((1,), (1,)), ((), ())), preferred_element_type=f32
+            )
+            logits = part if logits is None else logits + part
+        logits = jax.nn.sigmoid(logits + bo_ref[...])
+        for j in range(2):
+            l_ref[j, pl.ds(pl.multiple_of(8 * h, 8), 8), :] = jnp.concatenate(
+                [logits[8 * q : 8 * q + 8, 128 * j : 128 * j + 128] for q in range(4)], axis=1
+            )
+        return carry
+
+    lax.fori_loop(0, H, decode, 0)
+
+    for j in range(2):
+        v = l_ref[j]
+        high = v.astype(bf)
+        rest = (v - high.astype(f32)).astype(bf)
+        done = dot(high, join_ref[...]) + dot(rest, join_ref[...])
+        for h in range(H):
+            for px in range(2):
+                at = (2 * h + px) * E * E + 512 * j
+                out_ref[:, at : at + 512] = done[8 * h + 4 * px : 8 * h + 4 * px + 3]
+
+
+def flat_shards(
+    image,
+    context,
+    tissue,
+    owner,
+    neighbours,
+    w_in,
+    b_in,
+    w_down,
+    b_down,
+    w_ctx,
+    w_mid,
+    b_mid,
+    w_skip,
+    w_lift,
+    b_up,
+    w_out,
+    b_out,
+):
+    bf = jnp.bfloat16
+    count = lax.axis_size("blk")
+    half = count // 2
+    nbr = neighbours[0, 0]
+    me = lax.axis_index("blk")
+    pos = jnp.sum(jnp.where(owner[0] == me, tissue[0], 0))
+    have = (nbr >= 0).astype(jnp.int32)
+    scalars = jnp.concatenate([jnp.stack([pos // 4, pos % 4]), have]).astype(jnp.int32)
+
+    img = image.reshape(E, E * E)
+    face = jnp.where(nbr[0] >= 0, img[:REACH], img[E - REACH :])
+    face = lax.ppermute(face, "blk", [(i, (i + half) % count) for i in range(count)])
+    zero = jnp.zeros_like(face)
+    ex = jnp.concatenate(
+        [jnp.where(nbr[0] >= 0, face, zero), img, jnp.where(nbr[1] >= 0, face, zero)], axis=0
+    )
+    ups = [(i, i + 1) for i in range(lax.axis_size("grp") - 1)]
+    below = lax.ppermute(context, "grp", ups)
+    above = lax.ppermute(context, "grp", [(j, i) for i, j in ups])
+    lo = from_behind(ex[:, (E - REACH) * E :], "blk", 1)
+    hi = from_behind(ex[:, : REACH * E], "blk", -1)
+    lo = jnp.where(nbr[2] >= 0, lo, jnp.zeros_like(lo))
+    hi = jnp.where(nbr[3] >= 0, hi, jnp.zeros_like(hi))
+
+    rows, split, join = selections()
+    c0, c1 = w_skip.shape[1], w_skip.shape[0]
+    w1 = input_taps(w_in)
+    b1 = jnp.tile(b_in, 8)[None, :]
+    wd = jnp.swapaxes(w_down, 1, 2)
+    wd = jnp.concatenate([wd[1:], wd[:1]], axis=0).reshape(7 * c0, c1)
+    wm = jnp.swapaxes(w_mid, 1, 2)
+    wm = jnp.concatenate([wm[1:], wm[:1]], axis=0).reshape(7 * c1, c1)
+    skip, lift = w_skip.T, w_lift.T
+    none = jnp.zeros_like(skip)
+    wp = jnp.concatenate(
+        [
+            jnp.concatenate([skip, none], axis=1),
+            jnp.concatenate([none, skip], axis=1),
+            jnp.concatenate([lift, lift], axis=1),
+        ],
+        axis=0,
+    )
+    bp = jnp.tile(b_up, 2)[None, :]
+    wo = jnp.zeros((4, 32, 2 * c1), bf)
+    for m in range(4):
+        px, py = m // 2, m % 2
+        for pz in range(2):
+            at = (py * 2 + pz) * 8 + px * 4
+            wo = wo.at[m, at : at + 3, pz * c1 : (pz + 1) * c1].set(w_out)
+    bo = jnp.tile(jnp.concatenate([b_out, jnp.zeros((1,), jnp.float32)]), 8)[:, None]
+
+    grid4 = (16, 4, 16, context.shape[-1])
+    vmem = pl.BlockSpec(memory_space=pltpu.VMEM)
+    out = pl.pallas_call(
+        block_kernel,
+        out_shape=jax.ShapeDtypeStruct((3, E * E * E), jnp.float32),
+        in_specs=[pl.BlockSpec(memory_space=pltpu.SMEM)] + [vmem] * 20,
+        out_specs=vmem,
+        scratch_shapes=[
+            pltpu.VMEM((4, 8 * SLABS, 384), jnp.float32),
+            pltpu.VMEM((SLABS, 32, 384), jnp.float32),
+            pltpu.VMEM((H, 256, 512), bf),
+            pltpu.VMEM((SLABS, 320, 128), bf),
+            pltpu.VMEM((H + 2, 288, 128), bf),
+            pltpu.VMEM((48, 512), bf),
+            pltpu.VMEM((512, 128), bf),
+            pltpu.VMEM((4, 128, 128), bf),
+            pltpu.VMEM((2, 8 * H, 512), jnp.float32),
+        ],
+        compiler_params=pltpu.CompilerParams(vmem_limit_bytes=40 << 20),
+    )(
+        scalars, ex, lo, hi, rows, split, join,
+        context.reshape(grid4), below.reshape(grid4), above.reshape(grid4),
+        w1, b1, wd, b_down[None, :], w_ctx, wm, b_mid[None, :], wp, bp, wo, bo,
+    )
+    return out.reshape(1, 1, 3, E * E * E)
+
+
 def solution(mesh):
+    flat = mesh.shape["blk"] == 8
     return jax.shard_map(
-        shards,
+        flat_shards if flat else layered_shards,
         mesh=mesh,
         in_specs=(
             P("grp", "blk", None),

time: 191 us -> 67.8 us (0.35)
  other arithmetic: 57.4 us -> 3.2 us
  matrix products: 50.9 us -> 0 us
  starting transfers between devices: 39.2 us -> 11 us
  Pallas kernels: 0 us -> 25 us
  waiting for transfers between devices: 18 us -> 6.5 us
  local copies, waits for them, and re-layouts: 20.5 us -> 15.8 us
  between operations: 3.64 us -> 5.68 us
    dot_general x22 -> x0, matrix products: 50.9 us -> none  [the longest x1 34.8 us: shards(): jnp.dot(w_out, hidden, preferred_element_type=jnp.float32) + b_out[:, None]]
    convert_element_type x2 -> x3, other arithmetic: 35.5 us -> 1.03 us  [the longest x1 0.66 us: flat_shards(): have = (nbr >= 0).astype(jnp.int32)]
    ppermute x18 -> x2, starting transfers between devices: 34 us -> 2.39 us  [from_behind(): lax.ppermute(shard, axis, [(i, (i + by) % devices) for i in range(devices)])]
    pallas_call x0 -> x1, Pallas kernels: none -> 25 us  [flat_shards(): pl.pallas_call(block_kernel, out_shape=jax.ShapeDtypeStruct((3, E * E * E...]
    reduce_max x1 -> x0, other arithmetic: 13.6 us -> none  [pooled(): a0.reshape(a0.shape[0], half, 2, half, 2, half, 2).max(axis=(2, 4, 6))]
    ppermute x18 -> x2, waiting for transfers between devices: 18 us -> 6.49 us  [from_behind(): lax.ppermute(shard, axis, [(i, (i + by) % devices) for i in range(devices)])]
    broadcast_in_dim x2 -> x7, local copies, waits for them, and re-layouts: 11.2 us -> 0.67 us  [input_taps(): tap = jnp.repeat(jnp.array(table, jnp.int32), chans, axis=1)]
    unnamed x63 -> x47, local copies, waits for them, and re-layouts: 0.84 us -> 8.39 us
  transfers between devices with their start and end apart: 20 -> 5, of which waited for: 6 -> 1; matrix products, arithmetic and copies ran while one was open for 40% -> 14% of each run, Pallas kernels for 0% -> 0%
where the time goes in v1:
time: 67.8 us; the launch traced here: 67.1 us
  Pallas kernels  25 us (37%)
  local copies, waits for them, and re-layouts  15.8 us (23%)
  starting transfers between devices  11 us (16%)
  waiting for transfers between devices  6.5 us (10%)
  between operations  5.68 us (8%)
  other arithmetic  3.2 us (5%)
    pallas_call x1, Pallas kernels, flat_shards(): pl.pallas_call(block_kernel, out_shape=jax.ShapeDtypeStruct((3, E * E * E...  25 us
    unnamed x47, local copies, waits for them, and re-layouts  8.39 us
    ppermute x2, waiting for transfers between devices, from_behind(): lax.ppermute(shard, axis, [(i, (i + by) % devices) for i in range(devices)])  6.49 us
    ppermute x1, starting transfers between devices, flat_shards(): lax.ppermute(face, 'blk', [(i, (i + half) % count) for i in range(count)])  4.13 us
    ppermute x1, starting transfers between devices, flat_shards(): below = lax.ppermute(context, 'grp', ups)  3.05 us
    ppermute x2, starting transfers between devices, from_behind(): lax.ppermute(shard, axis, [(i, (i + by) % devices) for i in range(devices)])  2.39 us
    scatter x8, local copies, waits for them, and re-layouts, flat_shards(): wo = wo.at[m, at:at + 3, pz * c1:(pz + 1) * c1].set(w_out)  2.2 us
    slice x1, local copies, waits for them, and re-layouts, flat_shards(): hi = jnp.where(nbr[3] >= 0, hi, jnp.zeros_like(hi))  1.48 us
  transfers between devices with their start and end apart: 5, of which 1 were waited for; matrix products, arithmetic and copies ran while one was open for 14% of the time, Pallas kernels for 0%

profile of v1, /device:TPU:0, one launch (start us, length us, event | category | flops | bytes accessed | tf_op | source)
XLA Modules:
  0.0 67.1 jit_solution(18435926909687493899)
XLA Ops:
  0.0 1.4 %collective-permute-start.4 = (bf16[1,1024,128]{2,1,0:T(8,128)(2,1)}, bf16[1,1024,128]{2,1,0:T(8,128)(2,1)S(1)}, u32[]{:S(2)}, u32[]{:S(2)}) collective-permute-start(bf16[1,1024,128]{2,1,0:T(8,128)(2,1)} %param.35), channel_id=1, source_target_pairs={{1,0},{2,1},{3,2},{5,4},{6,5},{7,6},{9,8},{10,9},{11,10},{13,12},{... | collective-permute-start | bytes 786440 | tf_op jit(solution)/shard_map/ppermute | solution.py:425
  1.4 3.1 %collective-permute-start.3 = (bf16[1,1024,128]{2,1,0:T(8,128)(2,1)}, bf16[1,1024,128]{2,1,0:T(8,128)(2,1)S(1)}, u32[]{:S(2)}, u32[]{:S(2)}) collective-permute-start(bf16[1,1024,128]{2,1,0:T(8,128)(2,1)} %param.35), channel_id=1, source_target_pairs={{0,1},{1,2},{2,3},{4,5},{5,6},{6,7},{8,9},{9,10},{10,11},{12,13},{... | collective-permute-start | bytes 786440 | tf_op jit(solution)/shard_map/ppermute | solution.py:424
  4.5 1.5 %fusion.39 = (s32[1,1,1]{2,1,0:T(1,128)}, s32[1,1,1]{2,1,0:T(1,128)}, s32[1,1,1]{2,1,0:T(1,128)}, s32[1,1,1]{2,1,0:T(1,128)}) fusion(s32[1,1,6]{2,1,0:T(1,128)} %param.38), kind=kLoop, calls=%fused_computation.89 | loop fusion | bytes 32 | tf_op jit(solution)/shard_map/slice | solution.py:429
  6.6 0.9 %fusion.8 = bf16[8192]{0:T(1024)(128)(2,1)S(1)} fusion(pred[]{:T(512)} %bitcast.3, bf16[1,1,32768]{2,1,0:T(2,128)(2,1)} %param.34), kind=kLoop, calls=%fused_computation.18 | loop fusion | flops 8192 | bytes 49153 | tf_op jit(solution)/shard_map/jit(_where)/select_n | solution.py:417
  7.5 4.1 %collective-permute-start = (bf16[8,1024]{1,0:T(8,128)(2,1)S(1)}, bf16[8,1024]{1,0:T(8,128)(2,1)S(1)}, u32[]{:S(2)}, u32[]{:S(2)}) collective-permute-start(bf16[8,1024]{1,0:T(8,128)(2,1)S(1)} %select_n.176), channel_id=1, source_target_pairs={{0,16},{4,20},{8,24},{12,28},{16,0},{20,4},{24,8},{28,12},{1,17},{... | collective-permute-start | bytes 49160 | tf_op jit(solution)/shard_map/ppermute | solution.py:418
  11.7 0.7 fusion.37
  12.4 0.6 copy-done.10
  13.8 0.6 copy-done.17
  14.6 0.6 copy-done.16
  15.4 0.6 copy-done.15
  16.2 0.6 copy-done.14
  17.0 0.6 copy-done.13
  17.8 0.6 copy-done.12
  18.6 0.6 copy-done.11
  19.8 0.4 copy-done.9
  20.3 0.6 copy-done.19
  20.9 0.6 fusion.36
  21.6 0.6 copy-done.21
  25.5 0.4 reduce.18
  26.0 2.3 %collective-permute-start.2 = (bf16[48,256]{1,0:T(8,128)(2,1)S(1)}, bf16[48,256]{1,0:T(8,128)(2,1)S(1)}, u32[]{:S(2)}, u32[]{:S(2)}) collective-permute-start(bf16[48,256]{1,0:T(8,128)(2,1)S(1)} %get-tuple-element.101), channel_id=1, source_target_pairs={{0,28},{4,0},{8,4},{12,8},{16,12},{20,16},{24,20},{28,24},{1,29},{... | collective-permute-start | bytes 73736 | tf_op jit(solution)/shard_map/ppermute | solution.py:13
  29.9 0.7 %copy-done.7 = bf16[3,128]{1,0:T(4,128)(2,1)S(1)} copy-done((bf16[3,128]{1,0:T(4,128)(2,1)S(1)}, bf16[3,128]{1,0:T(4,128)(2,1)}, u32[]{:S(2)}) %copy-start.7) | copy-done | bytes 792
  30.6 0.3 scatter.29
  30.9 0.3 scatter.30
  31.2 0.3 scatter.31
  31.5 0.3 scatter.34
  32.1 0.3 scatter.35
  32.4 0.3 scatter.36
  33.1 6.5 %collective-permute-done.1 = bf16[48,256]{1,0:T(8,128)(2,1)S(1)} collective-permute-done((bf16[48,256]{1,0:T(8,128)(2,1)S(1)}, bf16[48,256]{1,0:T(8,128)(2,1)S(1)}, u32[]{:S(2)}, u32[]{:S(2)}) %collective-permute-start.1) | collective-permute-done | bytes 24608 | tf_op jit(solution)/shard_map/ppermute | solution.py:13
  39.6 0.6 copy-done.22
  40.3 0.6 copy-done.2
  41.0 25.0 %shard_map.172 = f32[3,32768]{1,0:T(4,128)S(1)} custom-call(s32[8]{0:T(128)S(1)} %pad_add_fusion.s_ref, bf16[48,1024]{1,0:T(8,128)(2,1)S(1)} %pad_maximum_fusion.2.ex_ref, bf16[48,256]{1,0:T(8,128)(2,1)S(1)} %broadcast_select_fusion.2.lo_ref, bf16[48,256]{1,0:T(8,128)(2,1)S(1)} %broadcast_select_fusion.1.hi_ref, bf16[160,48]{1,0:T(8,128)(2,1)S(1)} %fusion.7.rows_ref, ...), custom_call_target="tpu_custom_call" | custom-call | tf_op jit(solution)/shard_map/pallas_call | solution.py:460
  65.9 1.2 %copy.26 = f32[1,1,3,32768]{3,1,2,0:T(1,128)} copy(f32[1,1,3,32768]{3,2,1,0:T(4,128)S(1)} %bitcast.43) | data formatting | bytes 786432 | tf_op jit(solution)/shard_map/reshape | solution.py:482
  (96 shorter events, 3.8 us)
Async XLA Ops:
  0.0 12.3 %copy-start.6 = (bf16[7,128,64]{1,2,0:T(8,128)(2,1)S(1)}, bf16[7,128,64]{1,2,0:T(8,128)(2,1)}, u32[]{:S(2)}) copy-start(bf16[7,128,64]{1,2,0:T(8,128)(2,1)} %param.41) | copy-start | bytes 344068
  0.0 12.4 %copy-start.5 = (bf16[7,128,128]{2,1,0:T(8,128)(2,1)S(1)}, bf16[7,128,128]{2,1,0:T(8,128)(2,1)}, u32[]{:S(2)}) copy-start(bf16[7,128,128]{2,1,0:T(8,128)(2,1)} %param.44) | copy-start | bytes 688132
  0.0 39.6 %collective-permute-start.4 = (bf16[1,1024,128]{2,1,0:T(8,128)(2,1)}, bf16[1,1024,128]{2,1,0:T(8,128)(2,1)S(1)}, u32[]{:S(2)}, u32[]{:S(2)}) collective-permute-start(bf16[1,1024,128]{2,1,0:T(8,128)(2,1)} %param.35), channel_id=1, source_target_pairs={{1,0},{2,1},{3,2},{5,4},{6,5},{7,6},{9,8},{10,9},{11,10},{13,12},{... | collective-permute-start | bytes 786440 | tf_op jit(solution)/shard_map/ppermute | solution.py:425
  1.4 38.2 %collective-permute-start.3 = (bf16[1,1024,128]{2,1,0:T(8,128)(2,1)}, bf16[1,1024,128]{2,1,0:T(8,128)(2,1)S(1)}, u32[]{:S(2)}, u32[]{:S(2)}) collective-permute-start(bf16[1,1024,128]{2,1,0:T(8,128)(2,1)} %param.35), channel_id=1, source_target_pairs={{0,1},{1,2},{2,3},{4,5},{5,6},{6,7},{8,9},{9,10},{10,11},{12,13},{... | collective-permute-start | bytes 786440 | tf_op jit(solution)/shard_map/ppermute | solution.py:424
  7.5 18.4 %collective-permute-start = (bf16[8,1024]{1,0:T(8,128)(2,1)S(1)}, bf16[8,1024]{1,0:T(8,128)(2,1)S(1)}, u32[]{:S(2)}, u32[]{:S(2)}) collective-permute-start(bf16[8,1024]{1,0:T(8,128)(2,1)S(1)} %select_n.176), channel_id=1, source_target_pairs={{0,16},{4,20},{8,24},{12,28},{16,0},{20,4},{24,8},{28,12},{1,17},{... | collective-permute-start | bytes 49160 | tf_op jit(solution)/shard_map/ppermute | solution.py:418
  12.4 0.7 %copy-start.10 = (bf16[7,64,1]{1,0,2:T(8,128)(2,1)S(1)}, bf16[7,64,1]{1,0,2:T(8,128)(2,1)}, u32[]{:S(2)}) copy-start(bf16[7,64,1]{1,0,2:T(8,128)(2,1)} %param.39) | copy-start | bytes 2692
  12.4 1.3 %copy-start.8 = (bf16[128,128]{1,0:T(8,128)(2,1)S(1)}, bf16[128,128]{1,0:T(8,128)(2,1)}, u32[]{:S(2)}) copy-start(bf16[128,128]{1,0:T(8,128)(2,1)} %param.47) | copy-start | bytes 98308
  13.7 0.7 %copy-start.17 = (pred[32,8]{1,0:T(32,128)(4,1)S(1)}, pred[32,8]{1,0:T(32,128)(4,1)}, u32[]{:S(2)}) copy-start(pred[32,8]{1,0:T(32,128)(4,1)} %constant.404) | copy-start | bytes 772
  14.5 0.7 %copy-start.16 = (pred[32,8]{1,0:T(32,128)(4,1)S(1)}, pred[32,8]{1,0:T(32,128)(4,1)}, u32[]{:S(2)}) copy-start(pred[32,8]{1,0:T(32,128)(4,1)} %constant.405) | copy-start | bytes 772
  15.3 0.7 %copy-start.15 = (pred[32,8]{1,0:T(32,128)(4,1)S(1)}, pred[32,8]{1,0:T(32,128)(4,1)}, u32[]{:S(2)}) copy-start(pred[32,8]{1,0:T(32,128)(4,1)} %constant.406) | copy-start | bytes 772
  16.1 0.7 %copy-start.14 = (pred[32,8]{1,0:T(32,128)(4,1)S(1)}, pred[32,8]{1,0:T(32,128)(4,1)}, u32[]{:S(2)}) copy-start(pred[32,8]{1,0:T(32,128)(4,1)} %constant.407) | copy-start | bytes 772
  16.9 0.7 %copy-start.13 = (pred[32,8]{1,0:T(32,128)(4,1)S(1)}, pred[32,8]{1,0:T(32,128)(4,1)}, u32[]{:S(2)}) copy-start(pred[32,8]{1,0:T(32,128)(4,1)} %constant.408) | copy-start | bytes 772
  17.7 0.7 %copy-start.12 = (pred[32,8]{1,0:T(32,128)(4,1)S(1)}, pred[32,8]{1,0:T(32,128)(4,1)}, u32[]{:S(2)}) copy-start(pred[32,8]{1,0:T(32,128)(4,1)} %constant.409) | copy-start | bytes 772
  18.5 0.7 %copy-start.11 = (pred[32,8]{1,0:T(32,128)(4,1)S(1)}, pred[32,8]{1,0:T(32,128)(4,1)}, u32[]{:S(2)}) copy-start(pred[32,8]{1,0:T(32,128)(4,1)} %constant.410) | copy-start | bytes 772
  19.5 0.7 %copy-start.9 = (bf16[128,64]{0,1:T(8,128)(2,1)S(1)}, bf16[128,64]{0,1:T(8,128)(2,1)}, u32[]{:S(2)}) copy-start(bf16[128,64]{0,1:T(8,128)(2,1)} %param.46) | copy-start | bytes 49156
  20.3 0.7 copy-start.19
  20.3 0.7 copy-start.20
  20.9 4.5 %copy-start.4 = (bf16[1,1,32768]{2,1,0:T(2,128)(2,1)S(1)}, bf16[1,1,32768]{2,1,0:T(2,128)(2,1)}, u32[]{:S(2)}) copy-start(bf16[1,1,32768]{2,1,0:T(2,128)(2,1)} %param.34) | copy-start | bytes 196612
  21.6 0.7 copy-start.21
  26.0 7.1 %collective-permute-start.2 = (bf16[48,256]{1,0:T(8,128)(2,1)S(1)}, bf16[48,256]{1,0:T(8,128)(2,1)S(1)}, u32[]{:S(2)}, u32[]{:S(2)}) collective-permute-start(bf16[48,256]{1,0:T(8,128)(2,1)S(1)} %get-tuple-element.101), channel_id=1, source_target_pairs={{0,28},{4,0},{8,4},{12,8},{16,12},{20,16},{24,20},{28,24},{1,29},{... | collective-permute-start | bytes 73736 | tf_op jit(solution)/shard_map/ppermute | solution.py:13
  29.1 0.7 copy-start.18
  29.9 0.7 %copy-start.7 = (bf16[3,128]{1,0:T(4,128)(2,1)S(1)}, bf16[3,128]{1,0:T(4,128)(2,1)}, u32[]{:S(2)}) copy-start(bf16[3,128]{1,0:T(4,128)(2,1)} %param.49) | copy-start | bytes 2308
  31.9 8.4 %copy-start = (bf16[1,1024,128]{2,1,0:T(8,128)(2,1)S(1)}, bf16[1,1024,128]{2,1,0:T(8,128)(2,1)}, u32[]{:S(2)}) copy-start(bf16[1,1024,128]{2,1,0:T(8,128)(2,1)} %param.35) | copy-start | bytes 786436
  31.9 8.4 %copy-start.1 = (bf16[7,128,128]{2,1,0:T(8,128)(2,1)S(1)}, bf16[7,128,128]{2,1,0:T(8,128)(2,1)}, u32[]{:S(2)}) copy-start(bf16[7,128,128]{2,1,0:T(8,128)(2,1)} %wc_ref.1) | copy-start | bytes 688132
  33.0 6.6 %collective-permute-start.1 = (bf16[48,256]{1,0:T(8,128)(2,1)S(1)}, bf16[48,256]{1,0:T(8,128)(2,1)S(1)}, u32[]{:S(2)}, u32[]{:S(2)}) collective-permute-start(bf16[48,256]{1,0:T(8,128)(2,1)S(1)} %get-tuple-element.102), channel_id=1, source_target_pairs={{0,4},{4,8},{8,12},{12,16},{16,20},{20,24},{24,28},{28,0},{1,5},{5... | collective-permute-start | bytes 73736 | tf_op jit(solution)/shard_map/ppermute | solution.py:13
  39.6 0.7 copy-start.22
  40.3 0.7 copy-start.2
  40.3 0.7 copy-start.3

commit v2 on v0

--- a/solution.py
+++ b/solution.py
@@ -1,6 +1,9 @@
 import jax
 import jax.numpy as jnp
+import numpy as np
 from jax import lax
+from jax.experimental import pallas as pl
+from jax.experimental.pallas import tpu as pltpu
 from jax.sharding import PartitionSpec as P
 
 E = 32
@@ -100,7 +103,7 @@
     return total.T.reshape(-1, coarse, coarse, coarse)
 
 
-def shards(
+def layered_shards(
     image,
     context,
     tissue,
@@ -151,9 +154,350 @@
     return jax.nn.sigmoid(logits).reshape(1, 1, 3, E * E * E)
 
 
+H = E // 2
+REACH = 8
+SLABS = H + 4
+WIDE = E + 2 * REACH
+
+
+def selections():
+    row = np.arange(8 * SLABS)
+    slab, kk = row // 8, row % 8
+    offset = np.where(kk < 4, kk - 1, kk % 2)
+    shift = np.where(kk < 4, 0, np.where(kk < 6, WIDE, 2 * WIDE))
+    pick = 2 * (slab - 2) + offset + REACH + shift
+    rows = pick[:, None] == np.arange(3 * WIDE)[None, :]
+    return jnp.asarray(rows, jnp.bfloat16)
+
+
+def tap_table(chans):
+    table = -np.ones((32, 8), np.int32)
+    for p in range(8):
+        px, py, pz = p // 4, p // 2 % 2, p % 2
+        same = (py * 2 + pz) * 8
+        other_y, other_z = ((1 - py) * 2 + pz) * 8, (py * 2 + 1 - pz) * 8
+        near, far_y, far_z = px + 1, 4 + px, 6 + px
+        table[same + near, p] = 0
+        table[same + px, p] = 1
+        table[same + px + 2, p] = 2
+        table[other_y + (far_y if py == 0 else near), p] = 3
+        table[other_y + (near if py == 0 else far_y), p] = 4
+        table[other_z + (far_z if pz == 0 else near), p] = 5
+        table[other_z + (near if pz == 0 else far_z), p] = 6
+    return jnp.asarray(np.repeat(table, chans, axis=1))
+
+
+def three_terms(v):
+    high = v.astype(jnp.bfloat16)
+    rest = v - high.astype(jnp.float32)
+    mid = rest.astype(jnp.bfloat16)
+    low = (rest - mid.astype(jnp.float32)).astype(jnp.bfloat16)
+    return [t.astype(jnp.float32) for t in (high, mid, low)]
+
+
+def block_kernel(
+    tissue_ref, owner_ref, nbr_ref, bo_ref,
+    ex_ref, lo_ref, hi_ref, rows_ref, ctx_ref, below_ref, above_ref,
+    win_hbm, b1_hbm, wdown_hbm, bd_hbm, wc_hbm, wmid_hbm, bm_hbm, skip_hbm, lift_hbm, bp_hbm, wout_hbm, tap_hbm,
+    out_ref,
+    win_ref, b1_ref, wdown_ref, bd_ref, wc_ref, wmid_ref, bm_ref, skip_ref, lift_ref, bp_ref, wout_ref, tap_ref,
+    sems, split_ref, p_ref, a0_ref, p1_ref, a1_ref, k1_ref, kd_ref, wm_ref, ku_ref, wp_ref, wo_ref, l_ref,
+):
+    bf, f32 = jnp.bfloat16, jnp.float32
+    copies = [
+        pltpu.make_async_copy(src, dst, sems.at[i])
+        for i, (src, dst) in enumerate(
+            (
+                (win_hbm, win_ref), (b1_hbm, b1_ref), (wdown_hbm, wdown_ref), (bd_hbm, bd_ref), (wc_hbm, wc_ref),
+                (wmid_hbm, wmid_ref), (bm_hbm, bm_ref), (skip_hbm, skip_ref), (lift_hbm, lift_ref),
+                (bp_hbm, bp_ref), (wout_hbm, wout_ref), (tap_hbm, tap_ref),
+            )
+        )
+    ]
+    for copy in copies:
+        copy.start()
+    me = lax.axis_index("blk")
+    pos = jnp.int32(0)
+    for j in range(tissue_ref.shape[1]):
+        pos = pos + jnp.where(owner_ref[0, j] == me, tissue_ref[0, j], 0)
+    bx, by = pos // 4, pos % 4
+    first = nbr_ref[0, 0] >= 0
+    second = nbr_ref[0, 1] >= 0
+    left, right = nbr_ref[0, 2] >= 0, nbr_ref[0, 3] >= 0
+
+    def iota(shape, dim):
+        return lax.broadcasted_iota(jnp.int32, shape, dim)
+
+    def dot(a, b):
+        return jnp.dot(a, b, preferred_element_type=f32)
+
+    for part in range(4):
+        cell = iota((128, 512), 0) + 128 * part
+        y, z = cell // E, cell % E
+        to = ((y % 2) * 2 + z % 2) * 128 + (y // 2) * H + z // 2
+        split_ref[128 * part : 128 * part + 128, :] = jnp.where(to == iota((128, 512), 1), 1.0, 0.0).astype(bf)
+
+    lo, hi = lo_ref[...].astype(f32), hi_ref[...].astype(f32)
+    lo = jnp.where(left, lo, 0.0)
+    hi = jnp.where(right, hi, 0.0)
+    field = jnp.concatenate([lo, ex_ref[...].astype(f32), hi], axis=1)
+    x = iota(field.shape, 0)
+    field = jnp.where((x >= jnp.where(first, 0, REACH)) & (x < jnp.where(second, WIDE, WIDE - REACH)), field, 0.0)
+    field = field.astype(bf)
+    parts = [dot(field[:, 512 * j : 512 * j + 512], split_ref[...]) for j in range(3)]
+    hz = iota((WIDE, 384), 1) % H
+    for q in range(4):
+        py, pz = q // 2, q % 2
+        v = jnp.concatenate([part[:, 128 * q : 128 * q + 128] for part in parts], axis=1)
+        ys = pltpu.roll(v, H if py == 1 else 384 - H, axis=1)
+        zs = pltpu.roll(v, 1 if pz == 1 else 383, axis=1)
+        zs = jnp.where(hz == (0 if pz == 1 else H - 1), 0.0, zs)
+        v = dot(rows_ref[...], jnp.concatenate([v.astype(bf), ys.astype(bf), zs.astype(bf)], axis=0))
+        p_ref[:, 8 * q : 8 * q + 8, :] = v.reshape(SLABS, 8, 384)
+
+    for copy in copies:
+        copy.wait()
+    taps = jnp.concatenate([win_ref[...].astype(f32)] * 8, axis=1)
+    tap = tap_ref[...]
+    w1 = jnp.zeros(tap.shape, f32)
+    for t in range(7):
+        w1 = jnp.where(tap == t, taps[t : t + 1], w1)
+    k1_ref[0:32, :] = w1.astype(bf)
+    b1 = jnp.concatenate([b1_ref[...]] * 8, axis=1)
+    k1_ref[32:48, :] = jnp.concatenate(three_terms(b1) + [jnp.zeros((13, 512), f32)], axis=0).astype(bf)
+    kd_ref[0:384, :] = wdown_ref[1:7].reshape(384, 128)
+    kd_ref[384:448, :] = wdown_ref[0]
+    kd_ref[448:512, :] = jnp.concatenate(
+        three_terms(bd_ref[...]) + [jnp.zeros((61, 128), f32)], axis=0
+    ).astype(bf)
+    for t in range(7):
+        wm_ref[128 * t : 128 * t + 128, :] = wmid_ref[(t + 1) % 7].T
+    skip, lift = skip_ref[...], lift_ref[...].T
+    none = jnp.zeros_like(skip)
+    wp_ref[0:64, :] = jnp.concatenate([skip, none], axis=1)
+    wp_ref[64:128, :] = jnp.concatenate([none, skip], axis=1)
+    wp_ref[128:256, :] = jnp.concatenate([lift, lift], axis=1)
+    head = jnp.concatenate([wout_ref[...].astype(f32), jnp.zeros((1, 128), f32)], axis=0)
+    head = jnp.concatenate([head] * 8, axis=0)
+    group = iota((32, 128), 0) // 4
+    for m in range(4):
+        px, py = m // 2, m % 2
+        wo_ref[m] = jnp.concatenate(
+            [jnp.where(group == (py * 2 + pz) * 2 + px, head, 0.0) for pz in range(2)], axis=1
+        ).astype(bf)
+    chan = iota((32, 256), 0) % 4
+    b_out = jnp.where(chan == 0, bo_ref[0], jnp.where(chan == 1, bo_ref[1], bo_ref[2]))
+
+    def near(dx, dy):
+        x, y = bx + dx, by + dy
+        ok = (x >= 0) & (x < 4) & (y >= 0) & (y < 4)
+        x, y = jnp.clip(x, 0, 3), jnp.clip(y, 0, 3)
+        v = ctx_ref[pl.ds(4 * x, 4), pl.ds(y, 1), :, :].reshape(64, 128)
+        return jnp.where(ok, v, jnp.zeros_like(v))
+
+    views = [near(0, 0), near(-1, 0), near(1, 0), near(0, -1), near(0, 1)]
+    for other in (below_ref, above_ref):
+        views.append(other[pl.ds(4 * bx, 4), pl.ds(by, 1), :, :].reshape(64, 128))
+    total = dot(views[0], wc_ref[0])
+    for t in range(1, 7):
+        total = total + dot(views[t], wc_ref[t])
+    terms = three_terms(total)
+    bias = three_terms(bm_ref[...])
+    for q in range(4):
+        ku_ref[q] = jnp.concatenate(
+            [t[16 * q : 16 * q + 16] for t in terms] + bias + [jnp.zeros((77, 128), f32)], axis=0
+        ).astype(bf)
+
+    ones = jnp.where(iota((16, 384), 0) < 3, 1.0, 0.0)
+    start = jnp.where(first, 0, 2)
+    p1_ref[0:2] = jnp.zeros((2, 320, 128), bf)
+    p1_ref[SLABS - 2 : SLABS] = jnp.zeros((2, 320, 128), bf)
+    a1_ref[0] = jnp.zeros((288, 128), bf)
+    a1_ref[H + 1] = jnp.zeros((288, 128), bf)
+
+    def keep(ok, v):
+        return jnp.where(ok, v, jnp.zeros_like(v))
+
+    def full_res(i, carry):
+        s = start + i
+        taps = jnp.concatenate([p_ref[s], ones], axis=0)
+        taps = taps.T[32:352].astype(bf)
+        a0 = jnp.maximum(dot(taps, k1_ref[...]).astype(bf), jnp.zeros((), bf))
+        a0_ref[s] = a0[32:288]
+        pool = jnp.maximum(
+            jnp.maximum(a0[:, 0:128], a0[:, 128:256]), jnp.maximum(a0[:, 256:384], a0[:, 384:512])
+        )
+        pool = jnp.maximum(pool, jnp.concatenate([pool[:, 64:128], pool[:, 0:64]], axis=1))
+        p1_ref[s, 0:32] = keep(left, pool[0:32])
+        p1_ref[s, 32:288] = pool[32:288]
+        p1_ref[s, 288:320] = keep(right, pool[288:320])
+        return carry
+
+    lax.fori_loop(0, H + 2, full_res, 0, unroll=UNROLL[0])
+
+    lane = iota((288, 128), 1)
+    zrow = iota((288, 128), 0) % H
+    low = lane < 64
+    cut = zrow == jnp.where(low, 0, H - 1)
+    extra = jnp.where(lane < 67, 1.0, 0.0).astype(bf)
+    begin = jnp.where(first, 0, 1)
+
+    def half_res(i, carry):
+        u = begin + i
+        s = u + 1
+        mid = p1_ref[s, 16:304]
+        t1 = jnp.where(low, p1_ref[s - 1, 16:304], p1_ref[s + 1, 16:304])
+        t2 = jnp.where(low, p1_ref[s, 0:288], p1_ref[s, 32:320])
+        wide = mid.astype(f32)
+        t3 = jnp.where(low, pltpu.roll(wide, 1, axis=0), pltpu.roll(wide, 287, axis=0))
+        t3 = jnp.where(cut, 0.0, t3).astype(bf)
+        t4 = jnp.where(low, mid, extra)
+        pre = dot(jnp.concatenate([t1, t2, t3, t4], axis=1), kd_ref[...])
+        a1 = jnp.maximum(pre, 0.0).astype(bf)
+        a1_ref[u, 0:16] = keep(left, a1[0:16])
+        a1_ref[u, 16:272] = a1[16:272]
+        a1_ref[u, 272:288] = keep(right, a1[272:288])
+        return carry
+
+    lax.fori_loop(0, H + 1, half_res, 0, unroll=UNROLL[1])
+
+    rows = iota((256, 128), 0)
+    cols = iota((256, 128), 1)
+    coarse = (rows // H) // 4 * 4 + rows % H // 4
+    spread = jnp.where(cols < 48, jnp.where(cols % H == coarse, 1.0, 0.0), jnp.where(cols < 51, 1.0, 0.0))
+    spread = spread.astype(bf)
+    zfirst, zlast = rows % H == 0, rows % H == H - 1
+
+    def decode(h, carry):
+        u = h + 1
+        mid = a1_ref[u, 16:272]
+        wide = mid.astype(f32)
+        zm = jnp.where(zfirst, 0.0, pltpu.roll(wide, 1, axis=0)).astype(bf)
+        zp = jnp.where(zlast, 0.0, pltpu.roll(wide, 255, axis=0)).astype(bf)
+        field = jnp.concatenate(
+            [a1_ref[u - 1, 16:272], a1_ref[u + 1, 16:272], a1_ref[u, 0:256], a1_ref[u, 32:288], zm, zp, mid, spread],
+            axis=1,
+        )
+        pre = dot(field, jnp.concatenate([wm_ref[...], ku_ref[h // 4]], axis=0))
+        a2 = jnp.maximum(pre, 0.0).astype(bf)
+        logits = None
+        b_up = jnp.concatenate([bp_ref[...]] * 2, axis=1)
+        for m in range(4):
+            both = jnp.concatenate([a0_ref[h + 2, :, 128 * m : 128 * m + 128], a2], axis=1)
+            hidden = jnp.maximum((dot(both, wp_ref[...]) + b_up).astype(bf), jnp.zeros((), bf))
+            part = lax.dot_general(
+                wo_ref[m], hidden, (((1,), (1,)), ((), ())), preferred_element_type=f32
+            )
+            logits = part if logits is None else logits + part
+        logits = jax.nn.sigmoid(logits + b_out)
+        for j in range(2):
+            for q in range(4):
+                l_ref[j, q, pl.ds(pl.multiple_of(8 * h, 8), 8), :] = logits[
+                    8 * q : 8 * q + 8, 128 * j : 128 * j + 128
+                ]
+        return carry
+
+    lax.fori_loop(0, H, decode, 0, unroll=UNROLL[2])
+
+    v = jnp.concatenate(
+        [
+            jnp.concatenate([l_ref[j, q, pl.ds(c, E, stride=4), :] for q in range(4)], axis=1)
+            for j in range(2)
+            for c in range(3)
+        ],
+        axis=0,
+    )
+    high = v.astype(bf)
+    rest = (v - high.astype(f32)).astype(bf)
+
+    def back(t):
+        return lax.dot_general(t, split_ref[...], (((1,), (1,)), ((), ())), preferred_element_type=f32)
+
+    done = back(high) + back(rest)
+    for j in range(2):
+        for c in range(3):
+            at = E * (3 * j + c)
+            for b in range(4):
+                out_ref[pl.ds(256 * c + 4 * j + b, E, stride=8), :] = done[at : at + E, 128 * b : 128 * b + 128]
+
+
+UNROLL = (2, 1, 2)
+
+
+def flat_shards(
+    image,
+    context,
+    tissue,
+    owner,
+    neighbours,
+    w_in,
+    b_in,
+    w_down,
+    b_down,
+    w_ctx,
+    w_mid,
+    b_mid,
+    w_skip,
+    w_lift,
+    b_up,
+    w_out,
+    b_out,
+):
+    bf = jnp.bfloat16
+    count = lax.axis_size("blk")
+    half = count // 2
+    img = image.reshape(E, E * E)
+    face = jnp.concatenate([img[E - REACH :], img[:REACH]], axis=0)
+    face = lax.ppermute(face, "blk", [(i, (i + half) % count) for i in range(count)])
+    ex = jnp.concatenate([face[:REACH], img, face[REACH:]], axis=0)
+    lo = from_behind(ex[:, (E - REACH) * E :], "blk", 1)
+    hi = from_behind(ex[:, : REACH * E], "blk", -1)
+    ups = [(i, i + 1) for i in range(lax.axis_size("grp") - 1)]
+    below = lax.ppermute(context, "grp", ups)
+    above = lax.ppermute(context, "grp", [(j, i) for i, j in ups])
+
+    rows = selections()
+    grid4 = (16, 4, 16, context.shape[-1])
+    vmem = pl.BlockSpec(memory_space=pltpu.VMEM)
+    smem = pl.BlockSpec(memory_space=pltpu.SMEM)
+    operands = (
+        tissue, owner, neighbours[0], b_out,
+        ex, lo, hi, rows,
+        context.reshape(grid4), below.reshape(grid4), above.reshape(grid4),
+        w_in[:, :, 0], b_in[None, :], jnp.swapaxes(w_down, 1, 2), b_down[None, :],
+        w_ctx, w_mid, b_mid[None, :], w_skip.T, w_lift, b_up[None, :], w_out, tap_table(w_in.shape[1]),
+    )
+    held = operands[11:]
+    out = pl.pallas_call(
+        block_kernel,
+        out_shape=jax.ShapeDtypeStruct((3 * E * E * E // 128, 128), jnp.float32),
+        in_specs=[smem] * 4 + [vmem] * 7 + [pl.BlockSpec(memory_space=pltpu.HBM)] * len(held),
+        out_specs=vmem,
+        scratch_shapes=[pltpu.VMEM(v.shape, v.dtype) for v in held]
+        + [
+            pltpu.SemaphoreType.DMA((len(held),)),
+            pltpu.VMEM((512, 512), bf),
+            pltpu.VMEM((SLABS, 32, 384), jnp.float32),
+            pltpu.VMEM((SLABS, 256, 512), bf),
+            pltpu.VMEM((SLABS, 320, 128), bf),
+            pltpu.VMEM((H + 2, 288, 128), bf),
+            pltpu.VMEM((48, 512), bf),
+            pltpu.VMEM((512, 128), bf),
+            pltpu.VMEM((896, 128), bf),
+            pltpu.VMEM((4, 128, 128), bf),
+            pltpu.VMEM((256, 256), bf),
+            pltpu.VMEM((4, 32, 256), bf),
+            pltpu.VMEM((2, 4, 8 * H, 128), jnp.float32),
+        ],
+        compiler_params=pltpu.CompilerParams(vmem_limit_bytes=67043328),
+    )(*operands)
+    return out.reshape(1, 1, 3, E * E * E)
+
+
 def solution(mesh):
+    flat = mesh.shape["blk"] == 8
     return jax.shard_map(
-        shards,
+        flat_shards if flat else layered_shards,
         mesh=mesh,
         in_specs=(
             P("grp", "blk", None),

time: 191 us -> 44 us (0.23)
  other arithmetic: 57.4 us -> 0.38 us
  matrix products: 50.9 us -> 0 us
  starting transfers between devices: 39.2 us -> 11.4 us
  Pallas kernels: 0 us -> 23.5 us
  local copies, waits for them, and re-layouts: 20.5 us -> 1.7 us
  waiting for transfers between devices: 18 us -> 6.63 us
  between operations: 3.64 us -> 0.08 us
    dot_general x22 -> x0, matrix products: 50.9 us -> none  [the longest x1 34.8 us: shards(): jnp.dot(w_out, hidden, preferred_element_type=jnp.float32) + b_out[:, None]]
    convert_element_type x2 -> x0, other arithmetic: 35.5 us -> none  [the longest x1 34.8 us: shards(): a0 = jnp.maximum(pre, 0.0).astype(jnp.bfloat16).reshape(-1, E, E, E)]
    ppermute x18 -> x2, starting transfers between devices: 34 us -> 2.28 us  [from_behind(): lax.ppermute(shard, axis, [(i, (i + by) % devices) for i in range(devices)])]
    pallas_call x0 -> x1, Pallas kernels: none -> 23.5 us  [flat_shards(): pl.pallas_call(block_kernel, out_shape=jax.ShapeDtypeStruct((3 * E * E *...]
    reduce_max x1 -> x0, other arithmetic: 13.6 us -> none  [pooled(): a0.reshape(a0.shape[0], half, 2, half, 2, half, 2).max(axis=(2, 4, 6))]
    ppermute x18 -> x2, waiting for transfers between devices: 18 us -> 6.63 us  [from_behind(): lax.ppermute(shard, axis, [(i, (i + by) % devices) for i in range(devices)])]
    broadcast_in_dim x2 -> x0, local copies, waits for them, and re-layouts: 11.2 us -> none  [upsample(): jnp.broadcast_to(v[:, :, None, :, None, :, None], (chans, side, factor, s...]
    ppermute x2 -> x3, starting transfers between devices: 5.15 us -> 9.14 us  [the longest x1 4.13 us: flat_shards(): lax.ppermute(face, 'blk', [(i, (i + half) % count) for i in range(count)])]
  transfers between devices with their start and end apart: 20 -> 5, of which waited for: 6 -> 2; matrix products, arithmetic and copies ran while one was open for 40% -> 1% of each run, Pallas kernels for 0% -> 0%
where the time goes in v2:
time: 44 us; the launch traced here: 43.7 us
  Pallas kernels  23.5 us (53%)
  starting transfers between devices  11.4 us (26%)
  waiting for transfers between devices  6.63 us (15%)
  local copies, waits for them, and re-layouts  1.7 us (4%)
    pallas_call x1, Pallas kernels, flat_shards(): pl.pallas_call(block_kernel, out_shape=jax.ShapeDtypeStruct((3 * E * E *...  23.5 us
    ppermute x2, waiting for transfers between devices, from_behind(): lax.ppermute(shard, axis, [(i, (i + by) % devices) for i in range(devices)])  6.63 us
    ppermute x1, starting transfers between devices, flat_shards(): lax.ppermute(face, 'blk', [(i, (i + half) % count) for i in range(count)])  4.13 us
    ppermute x1, starting transfers between devices, flat_shards(): below = lax.ppermute(context, 'grp', ups)  3.73 us
    ppermute x2, starting transfers between devices, from_behind(): lax.ppermute(shard, axis, [(i, (i + by) % devices) for i in range(devices)])  2.28 us
    ppermute x1, starting transfers between devices, flat_shards(): above = lax.ppermute(context, 'grp', [(j, i) for i, j in ups])  1.28 us
    slice x3, local copies, waits for them, and re-layouts, flat_shards(): face = jnp.concatenate([img[E - REACH:], img[:REACH]], axis=0)  1.03 us
  transfers between devices with their start and end apart: 5, of which 2 were waited for; matrix products, arithmetic and copies ran while one was open for 1% of the time, Pallas kernels for 0%

profile of v2, /device:TPU:0, one launch (start us, length us, event | category | flops | bytes accessed | tf_op | source)
XLA Modules:
  0.0 43.7 jit_solution(6341145252104819783)
XLA Ops:
  0.0 0.0 copy-start.1
  0.0 1.0 %slice_reduce_fusion.1 = (bf16[8192]{0:T(1024)(128)(2,1)S(1)}, bf16[8192]{0:T(1024)(128)(2,1)S(1)}) fusion(bf16[1,1,32768]{2,1,0:T(2,128)(2,1)} %param.19), kind=kLoop, calls=%fused_computation.3 | loop fusion | bytes 65536 | tf_op jit(solution)/shard_map/slice | solution.py:450
  1.1 4.1 %collective-permute-start = (bf16[16,1024]{1,0:T(8,128)(2,1)S(1)}, bf16[16,1024]{1,0:T(8,128)(2,1)S(1)}, u32[]{:S(2)}, u32[]{:S(2)}) collective-permute-start(bf16[16,1024]{1,0:T(8,128)(2,1)S(1)} %pad_maximum_fusion.1), channel_id=1, source_target_pairs={{0,16},{4,20},{8,24},{12,28},{16,0},{20,4},{24,8},{28,12},{1,17},{... | collective-permute-start | bytes 98312 | tf_op jit(solution)/shard_map/ppermute | solution.py:451
  5.2 1.3 %collective-permute-start.4 = (bf16[1,1024,128]{2,1,0:T(8,128)(2,1)}, bf16[1,1024,128]{2,1,0:T(8,128)(2,1)}, u32[]{:S(2)}, u32[]{:S(2)}) collective-permute-start(bf16[1,1024,128]{2,1,0:T(8,128)(2,1)} %param.20), channel_id=1, source_target_pairs={{1,0},{2,1},{3,2},{5,4},{6,5},{7,6},{9,8},{10,9},{11,10},{13,12},{... | collective-permute-start | bytes 786440 | tf_op jit(solution)/shard_map/ppermute | solution.py:457
  6.5 3.7 %collective-permute-start.3 = (bf16[1,1024,128]{2,1,0:T(8,128)(2,1)}, bf16[1,1024,128]{2,1,0:T(8,128)(2,1)}, u32[]{:S(2)}, u32[]{:S(2)}) collective-permute-start(bf16[1,1024,128]{2,1,0:T(8,128)(2,1)} %param.20), channel_id=1, source_target_pairs={{0,1},{1,2},{2,3},{4,5},{5,6},{6,7},{8,9},{9,10},{10,11},{12,13},{... | collective-permute-start | bytes 786440 | tf_op jit(solution)/shard_map/ppermute | solution.py:456
  10.2 0.0 copy-done.1
  10.2 0.4 reduce.2
  10.6 0.0 collective-permute-done
  10.7 0.0 copy-start
  10.7 0.6 %copy-done = bf16[48,1024]{1,0:T(8,128)(2,1)} copy-done((bf16[48,1024]{1,0:T(8,128)(2,1)}, bf16[48,1024]{1,0:T(8,128)(2,1)S(1)}, u32[]{:S(2)}) %copy-start) | copy-done | bytes 98328
  11.3 2.3 %collective-permute-start.2 = (bf16[48,256]{1,0:T(8,128)(2,1)S(1)}, bf16[48,256]{1,0:T(8,128)(2,1)}, u32[]{:S(2)}, u32[]{:S(2)}) collective-permute-start(bf16[48,256]{1,0:T(8,128)(2,1)S(1)} %get-tuple-element.7), channel_id=1, source_target_pairs={{0,28},{4,0},{8,4},{12,8},{16,12},{20,16},{24,20},{28,24},{1,29},{... | collective-permute-start | bytes 73736 | tf_op jit(solution)/shard_map/ppermute | solution.py:14
  13.6 0.0 collective-permute-start.1
  13.6 1.7 %collective-permute-done.2.hi_ref = bf16[48,256]{1,0:T(8,128)(2,1)} collective-permute-done((bf16[48,256]{1,0:T(8,128)(2,1)S(1)}, bf16[48,256]{1,0:T(8,128)(2,1)}, u32[]{:S(2)}, u32[]{:S(2)}) %collective-permute-start.2) | collective-permute-done | bytes 24608 | tf_op jit(solution)/shard_map/ppermute | solution.py:14
  15.2 5.0 %collective-permute-done.1.lo_ref = bf16[48,256]{1,0:T(8,128)(2,1)} collective-permute-done((bf16[48,256]{1,0:T(8,128)(2,1)S(1)}, bf16[48,256]{1,0:T(8,128)(2,1)}, u32[]{:S(2)}, u32[]{:S(2)}) %collective-permute-start.1) | collective-permute-done | bytes 24608 | tf_op jit(solution)/shard_map/ppermute | solution.py:14
  20.2 0.0 collective-permute-done.4
  20.2 0.0 collective-permute-done.3
  20.2 23.5 %shard_map.181 = f32[768,128]{1,0:T(8,128)} custom-call(s32[1,8]{1,0:T(1,128)} %tissue_ref.1, s32[1,8]{1,0:T(1,128)} %owner_ref.1, s32[1,6]{1,0:T(1,128)} %bitcast.16, f32[3]{0:T(128)} %bo_ref.1, bf16[48,1024]{1,0:T(8,128)(2,1)} %copy-done, bf16[48,256]{1,0:T(8,128)(2,1)} %collective-permute-done.1.lo_ref, bf16[48,256]{1,0:T(8,128)(2,1)} %collective-permute-done.2.hi_ref, ...), custom_call_target="tpu_custom_call" | custom-call | tf_op jit(solution)/shard_map/pallas_call | solution.py:471
  (7 shorter events, 0.1 us)
Async XLA Ops:
  0.0 10.2 %copy-start.1 = (bf16[1,1,32768]{2,1,0:T(2,128)(2,1)S(1)}, bf16[1,1,32768]{2,1,0:T(2,128)(2,1)}, u32[]{:S(2)}) copy-start(bf16[1,1,32768]{2,1,0:T(2,128)(2,1)} %param.19) | copy-start | bytes 196612
  1.1 9.6 %collective-permute-start = (bf16[16,1024]{1,0:T(8,128)(2,1)S(1)}, bf16[16,1024]{1,0:T(8,128)(2,1)S(1)}, u32[]{:S(2)}, u32[]{:S(2)}) collective-permute-start(bf16[16,1024]{1,0:T(8,128)(2,1)S(1)} %pad_maximum_fusion.1), channel_id=1, source_target_pairs={{0,16},{4,20},{8,24},{12,28},{16,0},{20,4},{24,8},{28,12},{1,17},{... | collective-permute-start | bytes 98312 | tf_op jit(solution)/shard_map/ppermute | solution.py:451
  5.2 15.0 %collective-permute-start.4 = (bf16[1,1024,128]{2,1,0:T(8,128)(2,1)}, bf16[1,1024,128]{2,1,0:T(8,128)(2,1)}, u32[]{:S(2)}, u32[]{:S(2)}) collective-permute-start(bf16[1,1024,128]{2,1,0:T(8,128)(2,1)} %param.20), channel_id=1, source_target_pairs={{1,0},{2,1},{3,2},{5,4},{6,5},{7,6},{9,8},{10,9},{11,10},{13,12},{... | collective-permute-start | bytes 786440 | tf_op jit(solution)/shard_map/ppermute | solution.py:457
  6.5 13.7 %collective-permute-start.3 = (bf16[1,1024,128]{2,1,0:T(8,128)(2,1)}, bf16[1,1024,128]{2,1,0:T(8,128)(2,1)}, u32[]{:S(2)}, u32[]{:S(2)}) collective-permute-start(bf16[1,1024,128]{2,1,0:T(8,128)(2,1)} %param.20), channel_id=1, source_target_pairs={{0,1},{1,2},{2,3},{4,5},{5,6},{6,7},{8,9},{9,10},{10,11},{12,13},{... | collective-permute-start | bytes 786440 | tf_op jit(solution)/shard_map/ppermute | solution.py:456
  10.7 0.6 %copy-start = (bf16[48,1024]{1,0:T(8,128)(2,1)}, bf16[48,1024]{1,0:T(8,128)(2,1)S(1)}, u32[]{:S(2)}) copy-start(bf16[48,1024]{1,0:T(8,128)(2,1)S(1)} %pad_maximum_fusion.ex_ref) | copy-start | bytes 294916
  11.3 3.9 %collective-permute-start.2 = (bf16[48,256]{1,0:T(8,128)(2,1)S(1)}, bf16[48,256]{1,0:T(8,128)(2,1)}, u32[]{:S(2)}, u32[]{:S(2)}) collective-permute-start(bf16[48,256]{1,0:T(8,128)(2,1)S(1)} %get-tuple-element.7), channel_id=1, source_target_pairs={{0,28},{4,0},{8,4},{12,8},{16,12},{20,16},{24,20},{28,24},{1,29},{... | collective-permute-start | bytes 73736 | tf_op jit(solution)/shard_map/ppermute | solution.py:14
  13.6 6.6 %collective-permute-start.1 = (bf16[48,256]{1,0:T(8,128)(2,1)S(1)}, bf16[48,256]{1,0:T(8,128)(2,1)}, u32[]{:S(2)}, u32[]{:S(2)}) collective-permute-start(bf16[48,256]{1,0:T(8,128)(2,1)S(1)} %get-tuple-element.8), channel_id=1, source_target_pairs={{0,4},{4,8},{8,12},{12,16},{16,20},{20,24},{24,28},{28,0},{1,5},{5... | collective-permute-start | bytes 73736 | tf_op jit(solution)/shard_map/ppermute | solution.py:14

commit v3 on v2

--- a/solution.py
+++ b/solution.py
@@ -5,6 +5,7 @@
 from jax.experimental import pallas as pl
 from jax.experimental.pallas import tpu as pltpu
 from jax.sharding import PartitionSpec as P
+
 
 E = 32
 
@@ -197,11 +198,11 @@
 
 def block_kernel(
     tissue_ref, owner_ref, nbr_ref, bo_ref,
-    ex_ref, lo_ref, hi_ref, rows_ref, ctx_ref, below_ref, above_ref,
+    img_ref, other_ref, lo_ref, hi_ref, rows_ref, ctx_hbm, even_hbm, odd_hbm,
     win_hbm, b1_hbm, wdown_hbm, bd_hbm, wc_hbm, wmid_hbm, bm_hbm, skip_hbm, lift_hbm, bp_hbm, wout_hbm, tap_hbm,
     out_ref,
     win_ref, b1_ref, wdown_ref, bd_ref, wc_ref, wmid_ref, bm_ref, skip_ref, lift_ref, bp_ref, wout_ref, tap_ref,
-    sems, split_ref, p_ref, a0_ref, p1_ref, a1_ref, k1_ref, kd_ref, wm_ref, ku_ref, wp_ref, wo_ref, l_ref,
+    view_ref, view_sems, sems, split_ref, p_ref, a0_ref, p1_ref, a1_ref, k1_ref, kd_ref, wm_ref, ku_ref, wp_ref, wo_ref, l_ref, bup_ref, spread_ref,
 ):
     bf, f32 = jnp.bfloat16, jnp.float32
     copies = [
@@ -221,6 +222,16 @@
     for j in range(tissue_ref.shape[1]):
         pos = pos + jnp.where(owner_ref[0, j] == me, tissue_ref[0, j], 0)
     bx, by = pos // 4, pos % 4
+    oks = []
+    for t, (dx, dy) in enumerate(((0, 0), (-1, 0), (1, 0), (0, -1), (0, 1), (0, 0), (0, 0))):
+        x, y = bx + dx, by + dy
+        oks.append((x >= 0) & (x < 4) & (y >= 0) & (y < 4) if dx or dy else None)
+        x, y = jnp.clip(x, 0, 3), jnp.clip(y, 0, 3)
+        source = ctx_hbm if t < 5 else (even_hbm, odd_hbm)[t - 5]
+        copies.append(
+            pltpu.make_async_copy(source.at[pl.ds(4 * x, 4), pl.ds(y, 1)], view_ref.at[t], view_sems.at[t])
+        )
+        copies[-1].start()
     first = nbr_ref[0, 0] >= 0
     second = nbr_ref[0, 1] >= 0
     left, right = nbr_ref[0, 2] >= 0, nbr_ref[0, 3] >= 0
@@ -231,29 +242,36 @@
     def dot(a, b):
         return jnp.dot(a, b, preferred_element_type=f32)
 
+    cell = iota((512, 1), 0)
+    y, z = cell >> 5, cell & (E - 1)
+    to = ((y & 1) * 2 + (z & 1)) * 128 + (y >> 1) * H + (z >> 1)
     for part in range(4):
-        cell = iota((128, 512), 0) + 128 * part
-        y, z = cell // E, cell % E
-        to = ((y % 2) * 2 + z % 2) * 128 + (y // 2) * H + z // 2
-        split_ref[128 * part : 128 * part + 128, :] = jnp.where(to == iota((128, 512), 1), 1.0, 0.0).astype(bf)
+        at = slice(128 * part, 128 * part + 128)
+        split_ref[at, :] = jnp.where(to[at] == iota((128, 512), 1), 1.0, 0.0).astype(bf)
 
     lo, hi = lo_ref[...].astype(f32), hi_ref[...].astype(f32)
     lo = jnp.where(left, lo, 0.0)
     hi = jnp.where(right, hi, 0.0)
-    field = jnp.concatenate([lo, ex_ref[...].astype(f32), hi], axis=1)
+    none = jnp.zeros_like(lo)
+    other = other_ref[...].astype(f32)
+    mid = jnp.concatenate([other[E - REACH :], img_ref[...].astype(f32), other[:REACH]], axis=0)
+    field = jnp.concatenate([none, lo, mid, hi, none], axis=1)
     x = iota(field.shape, 0)
     field = jnp.where((x >= jnp.where(first, 0, REACH)) & (x < jnp.where(second, WIDE, WIDE - REACH)), field, 0.0)
     field = field.astype(bf)
-    parts = [dot(field[:, 512 * j : 512 * j + 512], split_ref[...]) for j in range(3)]
-    hz = iota((WIDE, 384), 1) % H
+    parts = [dot(field[:, 512 * j : 512 * j + 512], split_ref[...]) for j in range(4)]
+    hz = iota((WIDE, 512), 1) & (H - 1)
+    inner = iota((8 * SLABS, 128), 1) < 64
     for q in range(4):
         py, pz = q // 2, q % 2
         v = jnp.concatenate([part[:, 128 * q : 128 * q + 128] for part in parts], axis=1)
-        ys = pltpu.roll(v, H if py == 1 else 384 - H, axis=1)
-        zs = pltpu.roll(v, 1 if pz == 1 else 383, axis=1)
+        ys = pltpu.roll(v, H if py == 1 else 512 - H, axis=1)
+        zs = pltpu.roll(v, 1 if pz == 1 else 511, axis=1)
         zs = jnp.where(hz == (0 if pz == 1 else H - 1), 0.0, zs)
         v = dot(rows_ref[...], jnp.concatenate([v.astype(bf), ys.astype(bf), zs.astype(bf)], axis=0))
-        p_ref[:, 8 * q : 8 * q + 8, :] = v.reshape(SLABS, 8, 384)
+        p_ref[:, 8 * q : 8 * q + 8, 0:256] = v[:, 128:384].reshape(SLABS, 8, 256)
+        edge = jnp.where(inner, v[:, 384:512], v[:, 0:128])
+        p_ref[:, 8 * q : 8 * q + 8, 256:384] = edge.reshape(SLABS, 8, 128)
 
     for copy in copies:
         copy.wait()
@@ -262,142 +280,143 @@
     w1 = jnp.zeros(tap.shape, f32)
     for t in range(7):
         w1 = jnp.where(tap == t, taps[t : t + 1], w1)
-    k1_ref[0:32, :] = w1.astype(bf)
     b1 = jnp.concatenate([b1_ref[...]] * 8, axis=1)
-    k1_ref[32:48, :] = jnp.concatenate(three_terms(b1) + [jnp.zeros((13, 512), f32)], axis=0).astype(bf)
-    kd_ref[0:384, :] = wdown_ref[1:7].reshape(384, 128)
-    kd_ref[384:448, :] = wdown_ref[0]
-    kd_ref[448:512, :] = jnp.concatenate(
-        three_terms(bd_ref[...]) + [jnp.zeros((61, 128), f32)], axis=0
-    ).astype(bf)
+    k1_ref[...] = jnp.concatenate([w1] + three_terms(b1) + [jnp.zeros((13, 512), f32)], axis=0).T.astype(bf)
+    for j, pair in enumerate(((1, 2), (3, 4), (5, 6), (0, None))):
+        upper = wdown_ref[pair[0]].astype(f32)
+        if pair[1] is None:
+            lower = jnp.concatenate(three_terms(bd_ref[...]) + [jnp.zeros((61, 128), f32)], axis=0)
+        else:
+            lower = wdown_ref[pair[1]].astype(f32)
+        kd_ref[:, 128 * j : 128 * j + 128] = jnp.concatenate([upper, lower], axis=0).T.astype(bf)
     for t in range(7):
-        wm_ref[128 * t : 128 * t + 128, :] = wmid_ref[(t + 1) % 7].T
-    skip, lift = skip_ref[...], lift_ref[...].T
-    none = jnp.zeros_like(skip)
-    wp_ref[0:64, :] = jnp.concatenate([skip, none], axis=1)
-    wp_ref[64:128, :] = jnp.concatenate([none, skip], axis=1)
-    wp_ref[128:256, :] = jnp.concatenate([lift, lift], axis=1)
+        wm_ref[:, 128 * t : 128 * t + 128] = wmid_ref[(t + 1) % 7]
+    skip = skip_ref[...].astype(f32).T
+    skip = jnp.concatenate([skip, jnp.zeros_like(skip)], axis=1)
+    wp_ref[0:128, 0:128] = skip.astype(bf)
+    wp_ref[128:256, 0:128] = pltpu.roll(skip, 64, axis=1).astype(bf)
+    wp_ref[0:128, 128:256] = lift_ref[...]
+    wp_ref[128:256, 128:256] = lift_ref[...]
+    bup_ref[...] = jnp.broadcast_to(bp_ref[...], (128, 128)).T
     head = jnp.concatenate([wout_ref[...].astype(f32), jnp.zeros((1, 128), f32)], axis=0)
     head = jnp.concatenate([head] * 8, axis=0)
-    group = iota((32, 128), 0) // 4
+    group = iota((32, 128), 0) >> 2
     for m in range(4):
         px, py = m // 2, m % 2
-        wo_ref[m] = jnp.concatenate(
+        wo_ref[:, 256 * m : 256 * m + 256] = jnp.concatenate(
             [jnp.where(group == (py * 2 + pz) * 2 + px, head, 0.0) for pz in range(2)], axis=1
         ).astype(bf)
-    chan = iota((32, 256), 0) % 4
+    chan = iota((32, 256), 0) & 3
     b_out = jnp.where(chan == 0, bo_ref[0], jnp.where(chan == 1, bo_ref[1], bo_ref[2]))
 
-    def near(dx, dy):
-        x, y = bx + dx, by + dy
-        ok = (x >= 0) & (x < 4) & (y >= 0) & (y < 4)
-        x, y = jnp.clip(x, 0, 3), jnp.clip(y, 0, 3)
-        v = ctx_ref[pl.ds(4 * x, 4), pl.ds(y, 1), :, :].reshape(64, 128)
-        return jnp.where(ok, v, jnp.zeros_like(v))
-
-    views = [near(0, 0), near(-1, 0), near(1, 0), near(0, -1), near(0, 1)]
-    for other in (below_ref, above_ref):
-        views.append(other[pl.ds(4 * bx, 4), pl.ds(by, 1), :, :].reshape(64, 128))
+    views = []
+    for t in range(7):
+        v = view_ref[t].reshape(64, 128)
+        views.append(v if oks[t] is None else jnp.where(oks[t], v, jnp.zeros_like(v)))
     total = dot(views[0], wc_ref[0])
-    for t in range(1, 7):
+    for t in range(1, 5):
         total = total + dot(views[t], wc_ref[t])
+    odd = lax.axis_index("grp") % 2
+    total = total + dot(views[5], wc_ref[6 - odd]) + dot(views[6], wc_ref[5 + odd])
     terms = three_terms(total)
     bias = three_terms(bm_ref[...])
     for q in range(4):
         ku_ref[q] = jnp.concatenate(
             [t[16 * q : 16 * q + 16] for t in terms] + bias + [jnp.zeros((77, 128), f32)], axis=0
-        ).astype(bf)
+        ).T.astype(bf)
 
     ones = jnp.where(iota((16, 384), 0) < 3, 1.0, 0.0)
-    start = jnp.where(first, 0, 2)
-    p1_ref[0:2] = jnp.zeros((2, 320, 128), bf)
-    p1_ref[SLABS - 2 : SLABS] = jnp.zeros((2, 320, 128), bf)
-    a1_ref[0] = jnp.zeros((288, 128), bf)
-    a1_ref[H + 1] = jnp.zeros((288, 128), bf)
+    near_x, next_x = jnp.where(first, 1, H + 2), jnp.where(first, 0, H + 3)
+    zero = jnp.zeros((), bf)
 
     def keep(ok, v):
         return jnp.where(ok, v, jnp.zeros_like(v))
 
-    def full_res(i, carry):
-        s = start + i
-        taps = jnp.concatenate([p_ref[s], ones], axis=0)
-        taps = taps.T[32:352].astype(bf)
-        a0 = jnp.maximum(dot(taps, k1_ref[...]).astype(bf), jnp.zeros((), bf))
-        a0_ref[s] = a0[32:288]
-        pool = jnp.maximum(
-            jnp.maximum(a0[:, 0:128], a0[:, 128:256]), jnp.maximum(a0[:, 256:384], a0[:, 384:512])
+    def full_res(i):
+        slabs = (2 * i, 2 * i + 1)
+        at = (near_x, next_x) if 2 * i == H else (2 * i + 2, 2 * i + 3)
+        taps = [jnp.concatenate([p_ref[s], ones], axis=0).astype(bf) for s in at]
+        taps = jnp.concatenate([t[:, 0:256] for t in taps] + [t[:, 256:384] for t in taps], axis=1)
+        a0 = jnp.maximum(dot(k1_ref[...], taps).astype(bf), zero)
+        pool = a0[0:64]
+        for p in range(1, 8):
+            pool = jnp.maximum(pool, a0[64 * p : 64 * p + 64])
+        for k, s in enumerate(slabs):
+            if s < H:
+                a0_ref[s] = a0[:, 256 * k : 256 * k + 256]
+            edge = pool[:, 512 + 128 * k : 640 + 128 * k]
+            p1_ref[s, :, 0:128] = keep(left, edge)
+            p1_ref[s, :, 128:384] = pool[:, 256 * k : 256 * k + 256]
+            p1_ref[s, :, 384:512] = keep(right, edge)
+
+    def beside(ref, s, lanes):
+        if 0 < s < H - 1:
+            return ref[s - 1, :, lanes], ref[s + 1, :, lanes]
+        if s == 0:
+            return keep(first, ref[H, :, lanes]), ref[1, :, lanes]
+        if s == H - 1:
+            return ref[H - 2, :, lanes], keep(second, ref[H, :, lanes])
+        behind, inside = ref[H + 1, :, lanes], jnp.where(first, ref[0, :, lanes], ref[H - 1, :, lanes])
+        return jnp.where(first, behind, inside), jnp.where(first, inside, behind)
+
+    hz = iota((64, 512), 1) & (H - 1)
+    notfirst = jnp.where(hz == 0, 0.0, 1.0).astype(bf)
+    notlast = jnp.where(hz == H - 1, 0.0, 1.0).astype(bf)
+    extra = jnp.where(iota((64, 512), 0) < 3, 1.0, 0.0).astype(bf)
+
+    def half_res(s):
+        mid = p1_ref[s]
+        field = jnp.concatenate(
+            [
+                *beside(p1_ref, s, slice(0, 512)), pltpu.roll(mid, H, axis=1), pltpu.roll(mid, 512 - H, axis=1),
+                pltpu.roll(mid, 1, axis=1) * notfirst, pltpu.roll(mid, 511, axis=1) * notlast, mid, extra,
+            ],
+            axis=0,
         )
-        pool = jnp.maximum(pool, jnp.concatenate([pool[:, 64:128], pool[:, 0:64]], axis=1))
-        p1_ref[s, 0:32] = keep(left, pool[0:32])
-        p1_ref[s, 32:288] = pool[32:288]
-        p1_ref[s, 288:320] = keep(right, pool[288:320])
-        return carry
-
-    lax.fori_loop(0, H + 2, full_res, 0, unroll=UNROLL[0])
-
-    lane = iota((288, 128), 1)
-    zrow = iota((288, 128), 0) % H
-    low = lane < 64
-    cut = zrow == jnp.where(low, 0, H - 1)
-    extra = jnp.where(lane < 67, 1.0, 0.0).astype(bf)
-    begin = jnp.where(first, 0, 1)
-
-    def half_res(i, carry):
-        u = begin + i
-        s = u + 1
-        mid = p1_ref[s, 16:304]
-        t1 = jnp.where(low, p1_ref[s - 1, 16:304], p1_ref[s + 1, 16:304])
-        t2 = jnp.where(low, p1_ref[s, 0:288], p1_ref[s, 32:320])
-        wide = mid.astype(f32)
-        t3 = jnp.where(low, pltpu.roll(wide, 1, axis=0), pltpu.roll(wide, 287, axis=0))
-        t3 = jnp.where(cut, 0.0, t3).astype(bf)
-        t4 = jnp.where(low, mid, extra)
-        pre = dot(jnp.concatenate([t1, t2, t3, t4], axis=1), kd_ref[...])
-        a1 = jnp.maximum(pre, 0.0).astype(bf)
-        a1_ref[u, 0:16] = keep(left, a1[0:16])
-        a1_ref[u, 16:272] = a1[16:272]
-        a1_ref[u, 272:288] = keep(right, a1[272:288])
-        return carry
-
-    lax.fori_loop(0, H + 1, half_res, 0, unroll=UNROLL[1])
-
-    rows = iota((256, 128), 0)
-    cols = iota((256, 128), 1)
-    coarse = (rows // H) // 4 * 4 + rows % H // 4
-    spread = jnp.where(cols < 48, jnp.where(cols % H == coarse, 1.0, 0.0), jnp.where(cols < 51, 1.0, 0.0))
-    spread = spread.astype(bf)
-    zfirst, zlast = rows % H == 0, rows % H == H - 1
-
-    def decode(h, carry):
-        u = h + 1
-        mid = a1_ref[u, 16:272]
-        wide = mid.astype(f32)
-        zm = jnp.where(zfirst, 0.0, pltpu.roll(wide, 1, axis=0)).astype(bf)
-        zp = jnp.where(zlast, 0.0, pltpu.roll(wide, 255, axis=0)).astype(bf)
+        a1 = jnp.maximum(dot(kd_ref[...], field).astype(bf), zero)
+        a1_ref[s, :, 0:128] = keep(left, a1[:, 0:128])
+        a1_ref[s, :, 128:384] = a1[:, 128:384]
+        a1_ref[s, :, 384:512] = keep(right, a1[:, 384:512])
+
+    rows = iota((128, 256), 0)
+    cols = iota((128, 256), 1)
+    coarse = (cols >> 6) * 4 + ((cols & (H - 1)) >> 2)
+    spread = jnp.where(rows < 48, jnp.where((rows & (H - 1)) == coarse, 1.0, 0.0), jnp.where(rows < 51, 1.0, 0.0))
+    spread_ref[...] = spread.astype(bf)
+    hz = cols & (H - 1)
+    notfirst2 = jnp.where(hz == 0, 0.0, 1.0).astype(bf)
+    notlast2 = jnp.where(hz == H - 1, 0.0, 1.0).astype(bf)
+
+    def decode(h):
+        wide = a1_ref[h]
+        mid = wide[:, 128:384]
         field = jnp.concatenate(
-            [a1_ref[u - 1, 16:272], a1_ref[u + 1, 16:272], a1_ref[u, 0:256], a1_ref[u, 32:288], zm, zp, mid, spread],
-            axis=1,
+            [
+                *beside(a1_ref, h, slice(128, 384)),
+                pltpu.roll(wide, H, axis=1)[:, 128:384], pltpu.roll(wide, 512 - H, axis=1)[:, 128:384],
+                pltpu.roll(mid, 1, axis=1) * notfirst2, pltpu.roll(mid, 255, axis=1) * notlast2, mid, spread_ref[...],
+            ],
+            axis=0,
         )
-        pre = dot(field, jnp.concatenate([wm_ref[...], ku_ref[h // 4]], axis=0))
-        a2 = jnp.maximum(pre, 0.0).astype(bf)
-        logits = None
-        b_up = jnp.concatenate([bp_ref[...]] * 2, axis=1)
+        pre = dot(jnp.concatenate([wm_ref[...], ku_ref[h // 4]], axis=1), field)
+        a2 = jnp.maximum(pre.astype(bf), zero)
+        b_up = bup_ref[...]
+        b_up = jnp.concatenate([b_up, b_up], axis=1)
+        b_up = jnp.concatenate([b_up, b_up], axis=0)
+        hidden = []
         for m in range(4):
-            both = jnp.concatenate([a0_ref[h + 2, :, 128 * m : 128 * m + 128], a2], axis=1)
-            hidden = jnp.maximum((dot(both, wp_ref[...]) + b_up).astype(bf), jnp.zeros((), bf))
-            part = lax.dot_general(
-                wo_ref[m], hidden, (((1,), (1,)), ((), ())), preferred_element_type=f32
-            )
-            logits = part if logits is None else logits + part
+            both = jnp.concatenate([a0_ref[h, 128 * m : 128 * m + 128, :], a2], axis=0)
+            hidden.append(jnp.maximum((dot(wp_ref[...], both) + b_up).astype(bf), zero))
+        logits = dot(wo_ref[...], jnp.concatenate(hidden, axis=0))
         logits = jax.nn.sigmoid(logits + b_out)
         for j in range(2):
             for q in range(4):
-                l_ref[j, q, pl.ds(pl.multiple_of(8 * h, 8), 8), :] = logits[
+                l_ref[j, q, 8 * h : 8 * h + 8, :] = logits[
                     8 * q : 8 * q + 8, 128 * j : 128 * j + 128
                 ]
-        return carry
-
-    lax.fori_loop(0, H, decode, 0, unroll=UNROLL[2])
+
+    for stage, index in ORDER:
+        (full_res, half_res, decode)[stage](index)
 
     v = jnp.concatenate(
         [
@@ -421,7 +440,9 @@
                 out_ref[pl.ds(256 * c + 4 * j + b, E, stride=8), :] = done[at : at + E, 128 * b : 128 * b + 128]
 
 
-UNROLL = (2, 1, 2)
+ORDER = (
+    [(0, H // 2)] + [(0, i) for i in range(H // 2)] + [(1, H)] + [(1, s) for s in range(H)] + [(2, h) for h in range(H)]
+)
 
 
 def flat_shards(
@@ -447,14 +468,21 @@
     count = lax.axis_size("blk")
     half = count // 2
     img = image.reshape(E, E * E)
-    face = jnp.concatenate([img[E - REACH :], img[:REACH]], axis=0)
-    face = lax.ppermute(face, "blk", [(i, (i + half) % count) for i in range(count)])
-    ex = jnp.concatenate([face[:REACH], img, face[REACH:]], axis=0)
-    lo = from_behind(ex[:, (E - REACH) * E :], "blk", 1)
-    hi = from_behind(ex[:, : REACH * E], "blk", -1)
-    ups = [(i, i + 1) for i in range(lax.axis_size("grp") - 1)]
-    below = lax.ppermute(context, "grp", ups)
-    above = lax.ppermute(context, "grp", [(j, i) for i, j in ups])
+    other = lax.ppermute(img, "blk", [(i, (i + half) % count) for i in range(count)])
+    grp = lax.axis_size("grp")
+    pairs = [[pair for i in range(odd, grp - 1, 2) for pair in ((i, i + 1), (i + 1, i))] for odd in range(2)]
+    swaps = [lax.ppermute(context, "grp", pair) for pair in pairs]
+
+    def face(mid, side, lanes):
+        return jnp.concatenate([side[E - REACH :, lanes], mid[:, lanes], side[:REACH, lanes]], axis=0)
+
+    def turn(shard, by):
+        return lax.ppermute(shard, "blk", [(i, i // half * half + (i + by) % half) for i in range(count)])
+
+    high, low = slice((E - REACH) * E, E * E), slice(0, REACH * E)
+    place = lax.axis_index("blk") % half
+    lo = turn(jnp.where(place == half - 1, face(other, img, high), face(img, other, high)), 1)
+    hi = turn(jnp.where(place == 0, face(other, img, low), face(img, other, low)), -1)
 
     rows = selections()
     grid4 = (16, 4, 16, context.shape[-1])
@@ -462,34 +490,38 @@
     smem = pl.BlockSpec(memory_space=pltpu.SMEM)
     operands = (
         tissue, owner, neighbours[0], b_out,
-        ex, lo, hi, rows,
-        context.reshape(grid4), below.reshape(grid4), above.reshape(grid4),
+        img, other, lo, hi, rows,
+        context.reshape(grid4), swaps[0].reshape(grid4), swaps[1].reshape(grid4),
         w_in[:, :, 0], b_in[None, :], jnp.swapaxes(w_down, 1, 2), b_down[None, :],
         w_ctx, w_mid, b_mid[None, :], w_skip.T, w_lift, b_up[None, :], w_out, tap_table(w_in.shape[1]),
     )
-    held = operands[11:]
+    held = operands[12:]
     out = pl.pallas_call(
         block_kernel,
         out_shape=jax.ShapeDtypeStruct((3 * E * E * E // 128, 128), jnp.float32),
-        in_specs=[smem] * 4 + [vmem] * 7 + [pl.BlockSpec(memory_space=pltpu.HBM)] * len(held),
+        in_specs=[smem] * 4 + [vmem] * 5 + [pl.BlockSpec(memory_space=pltpu.HBM)] * (3 + len(held)),
         out_specs=vmem,
         scratch_shapes=[pltpu.VMEM(v.shape, v.dtype) for v in held]
         + [
+            pltpu.VMEM((7, 4, 1, 16, context.shape[-1]), bf),
+            pltpu.SemaphoreType.DMA((7,)),
             pltpu.SemaphoreType.DMA((len(held),)),
             pltpu.VMEM((512, 512), bf),
             pltpu.VMEM((SLABS, 32, 384), jnp.float32),
-            pltpu.VMEM((SLABS, 256, 512), bf),
-            pltpu.VMEM((SLABS, 320, 128), bf),
-            pltpu.VMEM((H + 2, 288, 128), bf),
-            pltpu.VMEM((48, 512), bf),
-            pltpu.VMEM((512, 128), bf),
-            pltpu.VMEM((896, 128), bf),
+            pltpu.VMEM((H, 512, 256), bf),
+            pltpu.VMEM((H + 2, 64, 512), bf),
+            pltpu.VMEM((H + 1, 128, 512), bf),
+            pltpu.VMEM((512, 48), bf),
+            pltpu.VMEM((128, 512), bf),
+            pltpu.VMEM((128, 896), bf),
             pltpu.VMEM((4, 128, 128), bf),
             pltpu.VMEM((256, 256), bf),
-            pltpu.VMEM((4, 32, 256), bf),
+            pltpu.VMEM((32, 1024), bf),
             pltpu.VMEM((2, 4, 8 * H, 128), jnp.float32),
+            pltpu.VMEM((128, 128), jnp.float32),
+            pltpu.VMEM((128, 256), bf),
         ],
-        compiler_params=pltpu.CompilerParams(vmem_limit_bytes=67043328),
+        compiler_params=pltpu.CompilerParams(vmem_limit_bytes=67043328 - (800 << 10)),
     )(*operands)
     return out.reshape(1, 1, 3, E * E * E)
 

time: 44 us -> 36 us (0.82)
  Pallas kernels: 23.5 us -> 15.1 us
  starting transfers between devices: 11.4 us -> 9.81 us
  waiting for transfers between devices: 6.63 us -> 8.02 us
  other arithmetic: 0.38 us -> 1.28 us
    pallas_call x1, Pallas kernels: 23.5 us -> 15.1 us  [flat_shards(): pl.pallas_call(block_kernel, out_shape=jax.ShapeDtypeStruct((3 * E * E *...]
    ppermute x5, starting transfers between devices: 11.4 us -> 9.81 us  [the longest x2 5.07 us: flat_shards(): swaps = [lax.ppermute(context, 'grp', pair) for pair in pairs]]
    ppermute x5, waiting for transfers between devices: 6.63 us -> 8.02 us  [the longest x2 4.04 us: turn(): lax.ppermute(shard, 'blk', [(i, i // half * half + (i + by) % half) for i...]
    slice x5 -> x4, local copies, waits for them, and re-layouts: 1.04 us -> 0.01 us  [the longest x2 0.01 us: face(): mid[:, lanes]]
    unnamed x1, other arithmetic: 0.37 us -> 1.26 us
    unnamed x4 -> x12, local copies, waits for them, and re-layouts: 0.63 us -> 1.38 us
  transfers between devices with their start and end apart: 5 -> 5, of which waited for: 2 -> 3; matrix products, arithmetic and copies ran while one was open for 1% -> 4% of each run, Pallas kernels for 0% -> 0%
where the time goes in v3:
time: 36 us; the launch traced here: 35.8 us
  Pallas kernels  15.1 us (42%)
  starting transfers between devices  9.81 us (27%)
  waiting for transfers between devices  8.02 us (22%)
  local copies, waits for them, and re-layouts  1.43 us (4%)
  other arithmetic  1.28 us (4%)
    pallas_call x1, Pallas kernels, flat_shards(): pl.pallas_call(block_kernel, out_shape=jax.ShapeDtypeStruct((3 * E * E *...  15.1 us
    ppermute x2, starting transfers between devices, flat_shards(): swaps = [lax.ppermute(context, 'grp', pair) for pair in pairs]  5.07 us
    ppermute x2, waiting for transfers between devices, turn(): lax.ppermute(shard, 'blk', [(i, i // half * half + (i + by) % half) for i...  4.04 us
    ppermute x1, waiting for transfers between devices, flat_shards(): lax.ppermute(img, 'blk', [(i, (i + half) % count) for i in range(count)])  3.97 us
    ppermute x1, starting transfers between devices, flat_shards(): lax.ppermute(img, 'blk', [(i, (i + half) % count) for i in range(count)])  2.65 us
    ppermute x2, starting transfers between devices, turn(): lax.ppermute(shard, 'blk', [(i, i // half * half + (i + by) % half) for i...  2.08 us
    unnamed x12, local copies, waits for them, and re-layouts  1.38 us
    unnamed x1, other arithmetic  1.26 us
  transfers between devices with their start and end apart: 5, of which 3 were waited for; matrix products, arithmetic and copies ran while one was open for 4% of the time, Pallas kernels for 0%

profile of v3, /device:TPU:0, one launch (start us, length us, event | category | flops | bytes accessed | tf_op | source)
XLA Modules:
  0.0 35.8 jit_solution(11536918564270992709)
XLA Ops:
  0.0 0.7 %collective-permute-start.4 = (bf16[1,1024,128]{2,1,0:T(8,128)(2,1)}, bf16[1,1024,128]{2,1,0:T(8,128)(2,1)S(1)}, u32[]{:S(2)}, u32[]{:S(2)}) collective-permute-start(bf16[1,1024,128]{2,1,0:T(8,128)(2,1)} %param.20), channel_id=1, source_target_pairs={{1,2},{2,1},{5,6},{6,5},{9,10},{10,9},{13,14},{14,13},{17,18},{18,... | collective-permute-start | bytes 786440 | tf_op jit(solution)/shard_map/ppermute | solution.py:474
  0.7 4.4 %collective-permute-start.3 = (bf16[1,1024,128]{2,1,0:T(8,128)(2,1)}, bf16[1,1024,128]{2,1,0:T(8,128)(2,1)S(1)}, u32[]{:S(2)}, u32[]{:S(2)}) collective-permute-start(bf16[1,1024,128]{2,1,0:T(8,128)(2,1)} %param.20), channel_id=1, source_target_pairs={{0,1},{1,0},{2,3},{3,2},{4,5},{5,4},{6,7},{7,6},{8,9},{9,8},{10,11... | collective-permute-start | bytes 786440 | tf_op jit(solution)/shard_map/ppermute | solution.py:474
  5.1 1.3 %reduce = bf16[32768]{0:T(1024)(128)(2,1)S(1)} reduce(bf16[1,1,32768]{2,1,0:T(2,128)(2,1)} %param.19, bf16[]{:T(256)} %constant.32), dimensions={0,1}, to_apply=%param.19.reduce_sub_computation | reduce | bytes 131074 | tf_op args[0]
  6.4 0.0 copy-start
  6.4 2.7 %collective-permute-start = (bf16[32,1024]{1,0:T(8,128)(2,1)S(1)}, bf16[32,1024]{1,0:T(8,128)(2,1)S(1)}, u32[]{:S(2)}, u32[]{:S(2)}) collective-permute-start(bf16[32,1024]{1,0:T(8,128)(2,1)S(1)} %reshape.15.img_ref), channel_id=1, source_target_pairs={{0,16},{4,20},{8,24},{12,28},{16,0},{20,4},{24,8},{28,12},{1,17},{... | collective-permute-start | bytes 196616 | tf_op jit(solution)/shard_map/ppermute | solution.py:471
  9.1 0.0 copy-done
  9.1 4.0 %collective-permute-done.other_ref = bf16[32,1024]{1,0:T(8,128)(2,1)S(1)} collective-permute-done((bf16[32,1024]{1,0:T(8,128)(2,1)S(1)}, bf16[32,1024]{1,0:T(8,128)(2,1)S(1)}, u32[]{:S(2)}, u32[]{:S(2)}) %collective-permute-start) | collective-permute-done | bytes 65568 | tf_op jit(solution)/shard_map/ppermute | solution.py:471
  13.0 0.0 copy-start.3
  13.1 0.6 %copy-done.3 = bf16[32,1024]{1,0:T(8,128)(2,1)} copy-done((bf16[32,1024]{1,0:T(8,128)(2,1)}, bf16[32,1024]{1,0:T(8,128)(2,1)S(1)}, u32[]{:S(2)}) %copy-start.3) | copy-done | bytes 65560
  13.7 1.3 %collective-permute-start.2 = (bf16[48,256]{1,0:T(8,128)(2,1)S(1)}, bf16[48,256]{1,0:T(8,128)(2,1)S(1)}, u32[]{:S(2)}, u32[]{:S(2)}) collective-permute-start(bf16[48,256]{1,0:T(8,128)(2,1)S(1)} %maximum_select_fusion.1), channel_id=1, source_target_pairs={{0,12},{4,0},{8,4},{12,8},{16,28},{20,16},{24,20},{28,24},{1,13},{... | collective-permute-start | bytes 73736 | tf_op jit(solution)/shard_map/ppermute | solution.py:480
  15.0 0.7 %collective-permute-start.1 = (bf16[48,256]{1,0:T(8,128)(2,1)S(1)}, bf16[48,256]{1,0:T(8,128)(2,1)S(1)}, u32[]{:S(2)}, u32[]{:S(2)}) collective-permute-start(bf16[48,256]{1,0:T(8,128)(2,1)S(1)} %maximum_select_fusion), channel_id=1, source_target_pairs={{0,4},{4,8},{8,12},{12,0},{16,20},{20,24},{24,28},{28,16},{1,5},{5... | collective-permute-start | bytes 73736 | tf_op jit(solution)/shard_map/ppermute | solution.py:480
  15.8 1.7 %collective-permute-done.2.hi_ref = bf16[48,256]{1,0:T(8,128)(2,1)S(1)} collective-permute-done((bf16[48,256]{1,0:T(8,128)(2,1)S(1)}, bf16[48,256]{1,0:T(8,128)(2,1)S(1)}, u32[]{:S(2)}, u32[]{:S(2)}) %collective-permute-start.2) | collective-permute-done | bytes 24608 | tf_op jit(solution)/shard_map/ppermute | solution.py:480
  17.5 0.0 copy-start.4
  17.5 2.3 %collective-permute-done.1.lo_ref = bf16[48,256]{1,0:T(8,128)(2,1)S(1)} collective-permute-done((bf16[48,256]{1,0:T(8,128)(2,1)S(1)}, bf16[48,256]{1,0:T(8,128)(2,1)S(1)}, u32[]{:S(2)}, u32[]{:S(2)}) %collective-permute-start.1) | collective-permute-done | bytes 24608 | tf_op jit(solution)/shard_map/ppermute | solution.py:480
  19.8 0.0 copy-start.5
  19.8 0.0 collective-permute-done.4
  19.8 0.0 copy-start.1
  19.8 0.0 collective-permute-done.3
  19.8 0.0 copy-start.2
  19.8 0.0 copy-done.4
  19.8 0.6 %copy-done.5 = bf16[48,256]{1,0:T(8,128)(2,1)} copy-done((bf16[48,256]{1,0:T(8,128)(2,1)}, bf16[48,256]{1,0:T(8,128)(2,1)S(1)}, u32[]{:S(2)}) %copy-start.5) | copy-done | bytes 24600
  20.4 0.1 copy-done.1
  20.5 0.1 copy-done.2
  20.6 15.1 %shard_map.181 = f32[768,128]{1,0:T(8,128)} custom-call(s32[1,8]{1,0:T(1,128)} %tissue_ref.1, s32[1,8]{1,0:T(1,128)} %owner_ref.1, s32[1,6]{1,0:T(1,128)} %bitcast.18, f32[3]{0:T(128)} %bo_ref.1, bf16[32,1024]{1,0:T(8,128)(2,1)} %copy-done, bf16[32,1024]{1,0:T(8,128)(2,1)} %copy-done.3, bf16[48,256]{1,0:T(8,128)(2,1)} %copy-done.5, ...), custom_call_target="tpu_custom_call" | custom-call | tf_op jit(solution)/shard_map/pallas_call | solution.py:499
  (7 shorter events, 0.1 us)
Async XLA Ops:
  0.0 19.8 %collective-permute-start.4 = (bf16[1,1024,128]{2,1,0:T(8,128)(2,1)}, bf16[1,1024,128]{2,1,0:T(8,128)(2,1)S(1)}, u32[]{:S(2)}, u32[]{:S(2)}) collective-permute-start(bf16[1,1024,128]{2,1,0:T(8,128)(2,1)} %param.20), channel_id=1, source_target_pairs={{1,2},{2,1},{5,6},{6,5},{9,10},{10,9},{13,14},{14,13},{17,18},{18,... | collective-permute-start | bytes 786440 | tf_op jit(solution)/shard_map/ppermute | solution.py:474
  0.7 19.1 %collective-permute-start.3 = (bf16[1,1024,128]{2,1,0:T(8,128)(2,1)}, bf16[1,1024,128]{2,1,0:T(8,128)(2,1)S(1)}, u32[]{:S(2)}, u32[]{:S(2)}) collective-permute-start(bf16[1,1024,128]{2,1,0:T(8,128)(2,1)} %param.20), channel_id=1, source_target_pairs={{0,1},{1,0},{2,3},{3,2},{4,5},{5,4},{6,7},{7,6},{8,9},{9,8},{10,11... | collective-permute-start | bytes 786440 | tf_op jit(solution)/shard_map/ppermute | solution.py:474
  6.4 2.7 %copy-start = (bf16[32,1024]{1,0:T(8,128)(2,1)}, bf16[32,1024]{1,0:T(8,128)(2,1)S(1)}, u32[]{:S(2)}) copy-start(bf16[32,1024]{1,0:T(8,128)(2,1)S(1)} %reshape.15.img_ref) | copy-start | bytes 196612
  6.4 6.6 %collective-permute-start = (bf16[32,1024]{1,0:T(8,128)(2,1)S(1)}, bf16[32,1024]{1,0:T(8,128)(2,1)S(1)}, u32[]{:S(2)}, u32[]{:S(2)}) collective-permute-start(bf16[32,1024]{1,0:T(8,128)(2,1)S(1)} %reshape.15.img_ref), channel_id=1, source_target_pairs={{0,16},{4,20},{8,24},{12,28},{16,0},{20,4},{24,8},{28,12},{1,17},{... | collective-permute-start | bytes 196616 | tf_op jit(solution)/shard_map/ppermute | solution.py:471
  13.0 0.6 %copy-start.3 = (bf16[32,1024]{1,0:T(8,128)(2,1)}, bf16[32,1024]{1,0:T(8,128)(2,1)S(1)}, u32[]{:S(2)}) copy-start(bf16[32,1024]{1,0:T(8,128)(2,1)S(1)} %collective-permute-done.other_ref) | copy-start | bytes 196612
  13.7 3.8 %collective-permute-start.2 = (bf16[48,256]{1,0:T(8,128)(2,1)S(1)}, bf16[48,256]{1,0:T(8,128)(2,1)S(1)}, u32[]{:S(2)}, u32[]{:S(2)}) collective-permute-start(bf16[48,256]{1,0:T(8,128)(2,1)S(1)} %maximum_select_fusion.1), channel_id=1, source_target_pairs={{0,12},{4,0},{8,4},{12,8},{16,28},{20,16},{24,20},{28,24},{1,13},{... | collective-permute-start | bytes 73736 | tf_op jit(solution)/shard_map/ppermute | solution.py:480
  15.0 4.8 %collective-permute-start.1 = (bf16[48,256]{1,0:T(8,128)(2,1)S(1)}, bf16[48,256]{1,0:T(8,128)(2,1)S(1)}, u32[]{:S(2)}, u32[]{:S(2)}) collective-permute-start(bf16[48,256]{1,0:T(8,128)(2,1)S(1)} %maximum_select_fusion), channel_id=1, source_target_pairs={{0,4},{4,8},{8,12},{12,0},{16,20},{20,24},{24,28},{28,16},{1,5},{5... | collective-permute-start | bytes 73736 | tf_op jit(solution)/shard_map/ppermute | solution.py:480
  17.5 2.3 %copy-start.4 = (bf16[48,256]{1,0:T(8,128)(2,1)}, bf16[48,256]{1,0:T(8,128)(2,1)S(1)}, u32[]{:S(2)}) copy-start(bf16[48,256]{1,0:T(8,128)(2,1)S(1)} %collective-permute-done.2.hi_ref) | copy-start | bytes 73732
  19.8 0.6 %copy-start.5 = (bf16[48,256]{1,0:T(8,128)(2,1)}, bf16[48,256]{1,0:T(8,128)(2,1)S(1)}, u32[]{:S(2)}) copy-start(bf16[48,256]{1,0:T(8,128)(2,1)S(1)} %collective-permute-done.1.lo_ref) | copy-start | bytes 73732
  19.8 0.7 %copy-start.1 = (bf16[1,1024,128]{2,1,0:T(8,128)(2,1)}, bf16[1,1024,128]{2,1,0:T(8,128)(2,1)S(1)}, u32[]{:S(2)}) copy-start(bf16[1,1024,128]{2,1,0:T(8,128)(2,1)S(1)} %collective-permute-done.4) | copy-start | bytes 786436
  19.8 0.8 %copy-start.2 = (bf16[1,1024,128]{2,1,0:T(8,128)(2,1)}, bf16[1,1024,128]{2,1,0:T(8,128)(2,1)S(1)}, u32[]{:S(2)}) copy-start(bf16[1,1024,128]{2,1,0:T(8,128)(2,1)S(1)} %collective-permute-done.3) | copy-start | bytes 786436
